TPU v7x, 256 devices: a whole 4x4x8 slice. The times are simulated.
256 devices in a mesh: ctx: 64 (over z, x, core), ch: 4 (over y).
Axes of the slice: x: 4, y: 4, z: 8, core: 2. Of those that a mesh axis runs over, the one named last changes fastest.
Arguments:
- signal: bfloat16 [32768, 1024], P('ctx', 'ch'), may hold values from -6 to 6
- gate_v: bfloat16 [32768, 1024], P('ctx', 'ch'), may hold values from -6 to 6
- taps: float32 [32768, 1024], P('ctx', 'ch'), may hold values from -1 to 1
- skip: float32 [1024], P('ch'), may hold values from -1 to 1
- norm_gain: float32 [1024], replicated, may hold values from 0.5 to 1.5
- router: float32 [1024, 32], replicated, may hold values from -0.1875 to 0.1875
- w_up: bfloat16 [64, 1024, 256], P('ctx'), may hold values from -0.1875 to 0.1875
- w_down: bfloat16 [64, 256, 1024], P('ctx'), may hold values from -0.25 to 0.25
- routes: int32 [32768, 2], P(('ctx', 'ch')), may hold values from 0 to 31, all different within a row; in each aligned block of 128 rows (0 to 127, 128 to 255, ...) at most 16 rows name the same one
Outputs:
- mixed: bfloat16 [32768, 1024], P('ctx', 'ch')
- moe_out: bfloat16 [32768, 1024], P('ctx', 'ch')
Inputs may be any that keep to these rules, and one draw needn't show every extreme that they name: `routes`: each row names two different experts. In each aligned block of 128 rows no expert is named by more than 16 rows.
All inputs are finite; a program needn't handle non-finite values.
Results may differ from a plain program's by a relative error of at most 0.017.
Values may be sent and summed in bfloat16 or wider, within the bound.
A program may use at most 64 MiB of HBM per device.

v0:
```python
import math

import jax
import jax.numpy as jnp
from jax import lax
from jax.sharding import PartitionSpec as P

CAP = 16


precise = lax.Precision.HIGHEST


def partner(block, axis, distance):
    count = lax.axis_size(axis)
    route = []
    for low in range(count):
        high = low | 1 << distance
        if high != low and high < count:
            route += [(low, high), (high, low)]
    return lax.ppermute(block, axis, route)


def dft_tables(length):
    index = jnp.arange(length, dtype=jnp.int32)
    angle = 2.0 * math.pi / length * (index[:, None] * index[None, :] % length).astype(jnp.float32)
    return (jnp.cos(angle), jnp.sin(angle))


def rotate(real_a, imag_a, real_b, imag_b):
    return (real_a * real_b - imag_a * imag_b, real_a * imag_b + imag_a * real_b)


def local_forward(real_part, imag_part, cosine, sine):
    out_real = jnp.matmul(real_part, cosine, precision=precise) + jnp.matmul(
        imag_part, sine, precision=precise
    )
    out_imag = jnp.matmul(imag_part, cosine, precision=precise) - jnp.matmul(
        real_part, sine, precision=precise
    )
    return (out_real, out_imag)


def local_inverse(real_part, imag_part, cosine, sine):
    count = cosine.shape[0]
    out_real = jnp.matmul(real_part, cosine, precision=precise) - jnp.matmul(
        imag_part, sine, precision=precise
    )
    out_imag = jnp.matmul(imag_part, cosine, precision=precise) + jnp.matmul(
        real_part, sine, precision=precise
    )
    return (out_real / count, out_imag / count)


def forward_pair(own_real, own_imag, far_real, far_imag, upper, tw_real, tw_imag):
    diff_real, diff_imag = rotate(far_real - own_real, far_imag - own_imag, tw_real, tw_imag)
    return (
        jnp.where(upper, diff_real, own_real + far_real),
        jnp.where(upper, diff_imag, own_imag + far_imag),
    )


def inverse_pair(own_real, own_imag, far_real, far_imag, upper, tw_real, tw_imag):
    first_real = jnp.where(upper, far_real, own_real)
    first_imag = jnp.where(upper, far_imag, own_imag)
    second_real = jnp.where(upper, own_real, far_real)
    second_imag = jnp.where(upper, own_imag, far_imag)
    turned_real, turned_imag = rotate(second_real, second_imag, tw_real, tw_imag)
    factor = jnp.where(upper, -0.5, 0.5)
    return (0.5 * first_real + factor * turned_real, 0.5 * first_imag + factor * turned_imag)


def body(signal, gate_v, taps, skip, norm_gain, router, w_up, w_down, routes):
    tok_dev, ch_dev = signal.shape
    shards = lax.axis_size("ctx")
    sections = shards.bit_length() - 1
    device = lax.axis_index("ctx")
    total = shards * tok_dev
    position = jnp.arange(tok_dev, dtype=jnp.int32)
    sig_float = signal.astype(jnp.float32)
    global_pos = (device * tok_dev + position).astype(jnp.float32)
    half_cos = jnp.cos(math.pi * global_pos / total)
    half_sin = jnp.sin(math.pi * global_pos / total)

    def lift(field):
        real_part = jnp.stack([field, field * half_cos], axis=1)
        imag_part = jnp.stack([jnp.zeros_like(field), -field * half_sin], axis=1)
        return (real_part, imag_part)

    sig_real, sig_imag = lift(sig_float.T)
    tap_real, tap_imag = lift(taps.T)
    cosine, sine = dft_tables(tok_dev)
    for level in reversed(range(sections)):
        span = 2**level * tok_dev
        offset = (device % 2**level * tok_dev + position).astype(jnp.float32)
        tw_real = jnp.cos(math.pi * offset / span)
        tw_imag = -jnp.sin(math.pi * offset / span)
        upper = device // 2**level % 2 == 1
        far = partner((sig_real, sig_imag, tap_real, tap_imag), "ctx", level)
        sig_real, sig_imag = forward_pair(
            sig_real, sig_imag, far[0], far[1], upper, tw_real, tw_imag
        )
        tap_real, tap_imag = forward_pair(
            tap_real, tap_imag, far[2], far[3], upper, tw_real, tw_imag
        )
    sig_real, sig_imag = local_forward(sig_real, sig_imag, cosine, sine)
    tap_real, tap_imag = local_forward(tap_real, tap_imag, cosine, sine)
    prod_real, prod_imag = rotate(sig_real, sig_imag, tap_real, tap_imag)
    prod_real, prod_imag = local_inverse(prod_real, prod_imag, cosine, sine)
    for level in range(sections):
        span = 2**level * tok_dev
        offset = (device % 2**level * tok_dev + position).astype(jnp.float32)
        tw_real = jnp.cos(math.pi * offset / span)
        tw_imag = jnp.sin(math.pi * offset / span)
        upper = device // 2**level % 2 == 1
        far = (
            partner(prod_real.astype(jnp.bfloat16), "ctx", level).astype(prod_real.dtype),
            partner(prod_imag.astype(jnp.bfloat16), "ctx", level).astype(prod_imag.dtype),
        )
        prod_real, prod_imag = inverse_pair(
            prod_real, prod_imag, far[0], far[1], upper, tw_real, tw_imag
        )
    low_half = 0.5 * (prod_real[:, 0] + prod_real[:, 1] * half_cos - prod_imag[:, 1] * half_sin)
    conv = low_half.T
    mixed = (gate_v.astype(jnp.float32) * (conv + skip * sig_float)).astype(jnp.bfloat16)
    full_rows = lax.all_to_all(mixed, "ch", split_axis=0, concat_axis=1, tiled=True)
    rows_float = full_rows.astype(jnp.float32)
    scale_row = lax.rsqrt(jnp.mean(rows_float * rows_float, axis=-1, keepdims=True) + 1e-05)
    normed = (rows_float * scale_row * norm_gain).astype(jnp.bfloat16)
    row_count, width = normed.shape
    num_experts = router.shape[1]
    logits = jnp.dot(normed.astype(jnp.float32), router, precision=precise)
    expert_ids = jnp.arange(num_experts, dtype=jnp.int32)
    picked_mask = routes[:, :, None] == expert_ids[None, None, :]
    gates = jax.nn.sigmoid(jnp.sum(jnp.where(picked_mask, logits[:, None, :], 0.0), axis=-1))
    flat_routes = routes.reshape(-1)
    flat_onehot = (flat_routes[:, None] == expert_ids[None, :]).astype(jnp.int32)
    slot_of = jnp.sum((jnp.cumsum(flat_onehot, axis=0) - flat_onehot) * flat_onehot, axis=-1)
    parts_dev = w_up.shape[0]
    part_ids = 2 * flat_routes[:, None] + jnp.arange(2, dtype=jnp.int32)[None, :]
    flat_pos = (
        part_ids // parts_dev * (parts_dev * CAP) + part_ids % parts_dev * CAP + slot_of[:, None]
    )
    flat_pos = flat_pos.reshape(-1)
    source_rows = jnp.repeat(jnp.arange(row_count, dtype=jnp.int32), 4)
    send_rows = (
        jnp.zeros((shards * parts_dev * CAP, width), jnp.bfloat16)
        .at[flat_pos]
        .set(normed[source_rows])
    )
    received = lax.all_to_all(
        send_rows.reshape(shards, parts_dev * CAP, width),
        "ctx",
        split_axis=0,
        concat_axis=0,
        tiled=True,
    )
    grouped = received.reshape(shards, parts_dev, CAP, width)
    hidden = jax.nn.gelu(
        jnp.einsum("spcd,pdh->spch", grouped, w_up, preferred_element_type=jnp.float32),
        approximate=True,
    ).astype(jnp.bfloat16)
    result = jnp.einsum(
        "spch,phd->spcd", hidden, w_down, preferred_element_type=jnp.float32
    ).astype(jnp.bfloat16)
    back = lax.all_to_all(
        result.reshape(shards, parts_dev * CAP, width),
        "ctx",
        split_axis=0,
        concat_axis=0,
        tiled=True,
    )
    picked = back.reshape(-1, width)[flat_pos].astype(jnp.float32).reshape(row_count, 2, 2, width)
    combined = jnp.sum(gates[:, :, None] * jnp.sum(picked, axis=2), axis=1)
    moe_rows = combined.astype(jnp.bfloat16)
    moe_out = lax.all_to_all(moe_rows, "ch", split_axis=1, concat_axis=0, tiled=True)
    return (mixed, moe_out)


def solution(mesh):
    in_specs = (
        P("ctx", "ch"),
        P("ctx", "ch"),
        P("ctx", "ch"),
        P("ch"),
        P(),
        P(),
        P("ctx", None, None),
        P("ctx", None, None),
        P(("ctx", "ch"), None),
    )
    out_specs = (P("ctx", "ch"), P("ctx", "ch"))
    return jax.shard_map(body, mesh=mesh, in_specs=in_specs, out_specs=out_specs, check_vma=False)
```

profile of v0, /device:TPU:1, one launch (start us, length us, event | category | flops | bytes accessed | tf_op | source)
XLA Modules:
  0.0 1132.5 jit_solution(200563703623152369)
XLA Ops:
  4.6 7.7 collective-permute-start
  21.0 20.0 %collective-permute-done = f32[256,2,512]{2,0,1:T(8,128)} collective-permute-done((f32[256,2,512]{2,0,1:T(8,128)}, f32[256,2,512]{2,0,1:T(8,128)}, u32[]{:S(2)}, u32[]{:S(2)}) %collective-permute-start) | collective-permute-done | bytes 1048608 | tf_op jit(solution)/shard_map/ppermute | solution.py:21
  41.0 32.6 %collective-permute-done.12 = f32[256,2,512]{2,0,1:T(8,128)} collective-permute-done((f32[256,2,512]{2,0,1:T(8,128)}, f32[256,2,512]{2,0,1:T(8,128)}, u32[]{:S(2)}, u32[]{:S(2)}) %collective-permute-start.12) | collective-permute-done | bytes 1048608 | tf_op jit(solution)/shard_map/ppermute | solution.py:21
  73.6 41.2 %collective-permute-done.1 = f32[256,2,512]{2,0,1:T(8,128)} collective-permute-done((f32[256,2,512]{2,0,1:T(8,128)}, f32[256,2,512]{2,0,1:T(8,128)}, u32[]{:S(2)}, u32[]{:S(2)}) %collective-permute-start.1) | collective-permute-done | bytes 1048608 | tf_op jit(solution)/shard_map/ppermute | solution.py:21
  114.8 50.6 %collective-permute-done.13 = f32[256,2,512]{2,0,1:T(8,128)} collective-permute-done((f32[256,2,512]{2,0,1:T(8,128)}, f32[256,2,512]{2,0,1:T(8,128)}, u32[]{:S(2)}, u32[]{:S(2)}) %collective-permute-start.13) | collective-permute-done | bytes 1048608 | tf_op jit(solution)/shard_map/ppermute | solution.py:21
  170.8 29.5 %collective-permute-start.14 = (f32[256,2,512]{2,0,1:T(8,128)}, f32[256,2,512]{2,0,1:T(8,128)S(1)}, u32[]{:S(2)}, u32[]{:S(2)}) collective-permute-start(f32[256,2,512]{2,0,1:T(8,128)} %get-tuple-element.58), channel_id=1, source_target_pairs={{0,64},{64,0},{4,68},{68,4},{8,72},{72,8},{12,76},{76,12},{16,80},... | collective-permute-start | bytes 3145736 | tf_op jit(solution)/shard_map/ppermute | solution.py:21
  202.7 109.2 %collective-permute-done.14 = f32[256,2,512]{2,0,1:T(8,128)S(1)} collective-permute-done((f32[256,2,512]{2,0,1:T(8,128)}, f32[256,2,512]{2,0,1:T(8,128)S(1)}, u32[]{:S(2)}, u32[]{:S(2)}) %collective-permute-start.14) | collective-permute-done | bytes 1048608 | tf_op jit(solution)/shard_map/ppermute | solution.py:21
  312.0 22.5 %collective-permute-done.15 = f32[256,2,512]{2,0,1:T(8,128)S(1)} collective-permute-done((f32[256,2,512]{2,0,1:T(8,128)}, f32[256,2,512]{2,0,1:T(8,128)S(1)}, u32[]{:S(2)}, u32[]{:S(2)}) %collective-permute-start.15) | collective-permute-done | bytes 1048608 | tf_op jit(solution)/shard_map/ppermute | solution.py:21
  334.4 22.6 %collective-permute-done.2 = f32[256,2,512]{2,0,1:T(8,128)} collective-permute-done((f32[256,2,512]{2,0,1:T(8,128)}, f32[256,2,512]{2,0,1:T(8,128)}, u32[]{:S(2)}, u32[]{:S(2)}) %collective-permute-start.2) | collective-permute-done | bytes 1048608 | tf_op jit(solution)/shard_map/ppermute | solution.py:21
  357.0 22.5 %collective-permute-done.3 = f32[256,2,512]{2,0,1:T(8,128)} collective-permute-done((f32[256,2,512]{2,0,1:T(8,128)}, f32[256,2,512]{2,0,1:T(8,128)}, u32[]{:S(2)}, u32[]{:S(2)}) %collective-permute-start.3) | collective-permute-done | bytes 1048608 | tf_op jit(solution)/shard_map/ppermute | solution.py:21
  379.5 6.2 add_select_fusion.10
  389.7 20.5 %collective-permute-done.16 = f32[256,2,512]{2,0,1:T(8,128)} collective-permute-done((f32[256,2,512]{2,0,1:T(8,128)S(1)}, f32[256,2,512]{2,0,1:T(8,128)}, u32[]{:S(2)}, u32[]{:S(2)}) %collective-permute-start.16) | collective-permute-done | bytes 1048608 | tf_op jit(solution)/shard_map/ppermute | solution.py:21
  410.2 22.5 %collective-permute-done.17 = f32[256,2,512]{2,0,1:T(8,128)} collective-permute-done((f32[256,2,512]{2,0,1:T(8,128)S(1)}, f32[256,2,512]{2,0,1:T(8,128)}, u32[]{:S(2)}, u32[]{:S(2)}) %collective-permute-start.17) | collective-permute-done | bytes 1048608 | tf_op jit(solution)/shard_map/ppermute | solution.py:21
  432.6 22.6 %collective-permute-done.4 = f32[256,2,512]{2,0,1:T(8,128)} collective-permute-done((f32[256,2,512]{2,0,1:T(8,128)}, f32[256,2,512]{2,0,1:T(8,128)}, u32[]{:S(2)}, u32[]{:S(2)}) %collective-permute-start.4) | collective-permute-done | bytes 1048608 | tf_op jit(solution)/shard_map/ppermute | solution.py:21
  455.2 22.5 %collective-permute-done.5 = f32[256,2,512]{2,0,1:T(8,128)} collective-permute-done((f32[256,2,512]{2,0,1:T(8,128)}, f32[256,2,512]{2,0,1:T(8,128)}, u32[]{:S(2)}, u32[]{:S(2)}) %collective-permute-start.5) | collective-permute-done | bytes 1048608 | tf_op jit(solution)/shard_map/ppermute | solution.py:21
  490.0 18.4 %collective-permute-done.18 = f32[256,2,512]{2,0,1:T(8,128)S(1)} collective-permute-done((f32[256,2,512]{2,0,1:T(8,128)}, f32[256,2,512]{2,0,1:T(8,128)S(1)}, u32[]{:S(2)}, u32[]{:S(2)}) %collective-permute-start.18) | collective-permute-done | bytes 1048608 | tf_op jit(solution)/shard_map/ppermute | solution.py:21
  508.3 22.5 %collective-permute-done.19 = f32[256,2,512]{2,0,1:T(8,128)S(1)} collective-permute-done((f32[256,2,512]{2,0,1:T(8,128)}, f32[256,2,512]{2,0,1:T(8,128)S(1)}, u32[]{:S(2)}, u32[]{:S(2)}) %collective-permute-start.19) | collective-permute-done | bytes 1048608 | tf_op jit(solution)/shard_map/ppermute | solution.py:21
  530.8 22.6 %collective-permute-done.6 = f32[256,2,512]{2,0,1:T(8,128)} collective-permute-done((f32[256,2,512]{2,0,1:T(8,128)}, f32[256,2,512]{2,0,1:T(8,128)}, u32[]{:S(2)}, u32[]{:S(2)}) %collective-permute-start.6) | collective-permute-done | bytes 1048608 | tf_op jit(solution)/shard_map/ppermute | solution.py:21
  553.4 22.5 %collective-permute-done.7 = f32[256,2,512]{2,0,1:T(8,128)} collective-permute-done((f32[256,2,512]{2,0,1:T(8,128)}, f32[256,2,512]{2,0,1:T(8,128)}, u32[]{:S(2)}, u32[]{:S(2)}) %collective-permute-start.7) | collective-permute-done | bytes 1048608 | tf_op jit(solution)/shard_map/ppermute | solution.py:21
  585.0 18.9 %collective-permute-done.20 = f32[256,2,512]{2,0,1:T(8,128)} collective-permute-done((f32[256,2,512]{2,0,1:T(8,128)S(1)}, f32[256,2,512]{2,0,1:T(8,128)}, u32[]{:S(2)}, u32[]{:S(2)}) %collective-permute-start.20) | collective-permute-done | bytes 1048608 | tf_op jit(solution)/shard_map/ppermute | solution.py:21
  603.9 22.5 %collective-permute-done.21 = f32[256,2,512]{2,0,1:T(8,128)} collective-permute-done((f32[256,2,512]{2,0,1:T(8,128)S(1)}, f32[256,2,512]{2,0,1:T(8,128)}, u32[]{:S(2)}, u32[]{:S(2)}) %collective-permute-start.21) | collective-permute-done | bytes 1048608 | tf_op jit(solution)/shard_map/ppermute | solution.py:21
  626.4 22.5 %collective-permute-done.8 = f32[256,2,512]{2,0,1:T(8,128)} collective-permute-done((f32[256,2,512]{2,0,1:T(8,128)}, f32[256,2,512]{2,0,1:T(8,128)}, u32[]{:S(2)}, u32[]{:S(2)}) %collective-permute-start.8) | collective-permute-done | bytes 1048608 | tf_op jit(solution)/shard_map/ppermute | solution.py:21
  648.8 22.5 %collective-permute-done.9 = f32[256,2,512]{2,0,1:T(8,128)} collective-permute-done((f32[256,2,512]{2,0,1:T(8,128)}, f32[256,2,512]{2,0,1:T(8,128)}, u32[]{:S(2)}, u32[]{:S(2)}) %collective-permute-start.9) | collective-permute-done | bytes 1048608 | tf_op jit(solution)/shard_map/ppermute | solution.py:21
  692.2 6.3 fusion.42
  698.6 6.3 fusion.38
  704.9 6.3 convolution_add_fusion.1
  711.2 6.5 fusion.44
  717.8 6.3 fusion.40
  724.1 6.3 convolution_add_fusion.2
  730.4 6.5 convolution_subtract_fusion.1
  737.0 6.5 multiply_subtract_fusion
  743.5 6.3 fusion.48
  749.8 6.7 fusion.46
  756.5 6.7 fusion.200
  763.6 6.7 fusion.199
  778.0 11.9 %collective-permute-done.26 = bf16[256,2,512]{2,0,1:T(8,128)(2,1)S(1)} collective-permute-done((bf16[256,2,512]{2,0,1:T(8,128)(2,1)}, bf16[256,2,512]{2,0,1:T(8,128)(2,1)S(1)}, u32[]{:S(2)}, u32[]{:S(2)}) %collective-permute-start.26) | collective-permute-done | bytes 524320 | tf_op jit(solution)/shard_map/ppermute | solution.py:21
  789.9 11.3 %collective-permute-done.27 = bf16[256,2,512]{2,0,1:T(8,128)(2,1)} collective-permute-done((bf16[256,2,512]{2,0,1:T(8,128)(2,1)}, bf16[256,2,512]{2,0,1:T(8,128)(2,1)}, u32[]{:S(2)}, u32[]{:S(2)}) %collective-permute-start.27) | collective-permute-done | bytes 524320 | tf_op jit(solution)/shard_map/ppermute | solution.py:21
  807.5 11.2 collective-permute-done.28
  818.6 11.2 collective-permute-done.29
  838.0 9.7 collective-permute-done.30
  847.6 11.2 collective-permute-done.31
  865.9 34.1 %collective-permute-done.32 = bf16[256,2,512]{2,0,1:T(8,128)(2,1)S(1)} collective-permute-done((bf16[256,2,512]{2,0,1:T(8,128)(2,1)}, bf16[256,2,512]{2,0,1:T(8,128)(2,1)S(1)}, u32[]{:S(2)}, u32[]{:S(2)}) %collective-permute-start.32) | collective-permute-done | bytes 524320 | tf_op jit(solution)/shard_map/ppermute | solution.py:21
  900.0 11.2 collective-permute-done.33
  923.1 43.0 %collective-permute-done.35 = bf16[256,2,512]{2,0,1:T(8,128)(2,1)S(1)} collective-permute-done((bf16[256,2,512]{2,0,1:T(8,128)(2,1)}, bf16[256,2,512]{2,0,1:T(8,128)(2,1)S(1)}, u32[]{:S(2)}, u32[]{:S(2)}) %collective-permute-start.35) | collective-permute-done | bytes 524320 | tf_op jit(solution)/shard_map/ppermute | solution.py:21
  979.3 6.8 scatter_custom_fusion
  986.2 60.6 %all_to_all.39 = bf16[64,16,1024]{2,1,0:T(8,128)(2,1)} all-to-all(bf16[64,16,1024]{2,1,0:T(8,128)(2,1)S(1)} %bitcast.171), channel_id=1, replica_groups=mesh['ctx'=64,'ch'=4] {'ctx'}, dimensions={0} | all-to-all | bytes 4194304 | tf_op jit(solution)/shard_map/all_to_all | solution.py:151
  1052.1 7.5 all-to-all-start.2
  1060.1 49.0 %all-to-all-done.2 = bf16[64,16,1024]{2,1,0:T(8,128)(2,1)S(1)} async-done(((bf16[64,16,1024]{2,1,0:T(8,128)(2,1)}), bf16[64,16,1024]{2,1,0:T(8,128)(2,1)S(1)}, u32[]{:S(2)}, u32[]{:S(2)}) %all-to-all-start.2) | async-done | bytes 2097184 | tf_op jit(solution)/shard_map/all_to_all | solution.py:166
  (152 shorter events, 149.7 us)
Async XLA Ops:
  0.6 1046.2 %copy-start = (bf16[1,256,1024]{2,1,0:T(8,128)(2,1)S(1)}, bf16[1,256,1024]{2,1,0:T(8,128)(2,1)}, u32[]{:S(2)}) copy-start(bf16[1,256,1024]{2,1,0:T(8,128)(2,1)} %param.16) | copy-start | bytes 1572868
  4.6 36.4 %collective-permute-start = (f32[256,2,512]{2,0,1:T(8,128)}, f32[256,2,512]{2,0,1:T(8,128)}, u32[]{:S(2)}, u32[]{:S(2)}) collective-permute-start(f32[256,2,512]{2,0,1:T(8,128)} %pad_maximum_fusion), channel_id=1, source_target_pairs={{0,128},{128,0},{4,132},{132,4},{8,136},{136,8},{12,140},{140,12},... | collective-permute-start | bytes 3145736 | tf_op jit(solution)/shard_map/ppermute | solution.py:21
  13.4 60.3 %collective-permute-start.12 = (f32[256,2,512]{2,0,1:T(8,128)}, f32[256,2,512]{2,0,1:T(8,128)}, u32[]{:S(2)}, u32[]{:S(2)}) collective-permute-start(f32[256,2,512]{2,0,1:T(8,128)} %pad_maximum_fusion.1), channel_id=1, source_target_pairs={{0,128},{128,0},{4,132},{132,4},{8,136},{136,8},{12,140},{140,12},... | collective-permute-start | bytes 3145736 | tf_op jit(solution)/shard_map/ppermute | solution.py:21
  14.5 100.3 %collective-permute-start.1 = (f32[256,2,512]{2,0,1:T(8,128)}, f32[256,2,512]{2,0,1:T(8,128)}, u32[]{:S(2)}, u32[]{:S(2)}) collective-permute-start(f32[256,2,512]{2,0,1:T(8,128)} %stack.34), channel_id=1, source_target_pairs={{0,128},{128,0},{4,132},{132,4},{8,136},{136,8},{12,140},{140,12},... | collective-permute-start | bytes 3145736 | tf_op jit(solution)/shard_map/ppermute | solution.py:21
  21.0 144.5 %collective-permute-start.13 = (f32[256,2,512]{2,0,1:T(8,128)}, f32[256,2,512]{2,0,1:T(8,128)}, u32[]{:S(2)}, u32[]{:S(2)}) collective-permute-start(f32[256,2,512]{2,0,1:T(8,128)} %stack.39), channel_id=1, source_target_pairs={{0,128},{128,0},{4,132},{132,4},{8,136},{136,8},{12,140},{140,12},... | collective-permute-start | bytes 3145736 | tf_op jit(solution)/shard_map/ppermute | solution.py:21
  170.8 141.1 %collective-permute-start.14 = (f32[256,2,512]{2,0,1:T(8,128)}, f32[256,2,512]{2,0,1:T(8,128)S(1)}, u32[]{:S(2)}, u32[]{:S(2)}) collective-permute-start(f32[256,2,512]{2,0,1:T(8,128)} %get-tuple-element.58), channel_id=1, source_target_pairs={{0,64},{64,0},{4,68},{68,4},{8,72},{72,8},{12,76},{76,12},{16,80},... | collective-permute-start | bytes 3145736 | tf_op jit(solution)/shard_map/ppermute | solution.py:21
  200.3 134.1 %collective-permute-start.15 = (f32[256,2,512]{2,0,1:T(8,128)}, f32[256,2,512]{2,0,1:T(8,128)S(1)}, u32[]{:S(2)}, u32[]{:S(2)}) collective-permute-start(f32[256,2,512]{2,0,1:T(8,128)} %get-tuple-element.59), channel_id=1, source_target_pairs={{0,64},{64,0},{4,68},{68,4},{8,72},{72,8},{12,76},{76,12},{16,80},... | collective-permute-start | bytes 3145736 | tf_op jit(solution)/shard_map/ppermute | solution.py:21
  200.3 156.7 %collective-permute-start.2 = (f32[256,2,512]{2,0,1:T(8,128)}, f32[256,2,512]{2,0,1:T(8,128)}, u32[]{:S(2)}, u32[]{:S(2)}) collective-permute-start(f32[256,2,512]{2,0,1:T(8,128)} %get-tuple-element.89), channel_id=1, source_target_pairs={{0,64},{64,0},{4,68},{68,4},{8,72},{72,8},{12,76},{76,12},{16,80},... | collective-permute-start | bytes 3145736 | tf_op jit(solution)/shard_map/ppermute | solution.py:21
  202.6 176.8 %collective-permute-start.3 = (f32[256,2,512]{2,0,1:T(8,128)}, f32[256,2,512]{2,0,1:T(8,128)}, u32[]{:S(2)}, u32[]{:S(2)}) collective-permute-start(f32[256,2,512]{2,0,1:T(8,128)} %get-tuple-element.90), channel_id=1, source_target_pairs={{0,64},{64,0},{4,68},{68,4},{8,72},{72,8},{12,76},{76,12},{16,80},... | collective-permute-start | bytes 3145736 | tf_op jit(solution)/shard_map/ppermute | solution.py:21
  311.9 67.5 %copy-start.2 = (f32[256,2,512]{2,0,1:T(8,128)}, f32[256,2,512]{2,0,1:T(8,128)S(1)}, u32[]{:S(2)}) copy-start(f32[256,2,512]{2,0,1:T(8,128)S(1)} %collective-permute-done.14) | copy-start | bytes 3145732
  334.4 45.1 %copy-start.4 = (f32[256,2,512]{2,0,1:T(8,128)}, f32[256,2,512]{2,0,1:T(8,128)S(1)}, u32[]{:S(2)}) copy-start(f32[256,2,512]{2,0,1:T(8,128)S(1)} %collective-permute-done.15) | copy-start | bytes 3145732
  385.7 24.5 %collective-permute-start.16 = (f32[256,2,512]{2,0,1:T(8,128)S(1)}, f32[256,2,512]{2,0,1:T(8,128)}, u32[]{:S(2)}, u32[]{:S(2)}) collective-permute-start(f32[256,2,512]{2,0,1:T(8,128)S(1)} %get-tuple-element.44), channel_id=1, source_target_pairs={{0,32},{32,0},{4,36},{36,4},{8,40},{40,8},{12,44},{44,12},{16,48},... | collective-permute-start | bytes 3145736 | tf_op jit(solution)/shard_map/ppermute | solution.py:21
  388.2 44.5 %collective-permute-start.17 = (f32[256,2,512]{2,0,1:T(8,128)S(1)}, f32[256,2,512]{2,0,1:T(8,128)}, u32[]{:S(2)}, u32[]{:S(2)}) collective-permute-start(f32[256,2,512]{2,0,1:T(8,128)S(1)} %get-tuple-element.45), channel_id=1, source_target_pairs={{0,32},{32,0},{4,36},{36,4},{8,40},{40,8},{12,44},{44,12},{16,48},... | collective-permute-start | bytes 3145736 | tf_op jit(solution)/shard_map/ppermute | solution.py:21
  388.2 67.0 %collective-permute-start.4 = (f32[256,2,512]{2,0,1:T(8,128)}, f32[256,2,512]{2,0,1:T(8,128)}, u32[]{:S(2)}, u32[]{:S(2)}) collective-permute-start(f32[256,2,512]{2,0,1:T(8,128)} %get-tuple-element.87), channel_id=1, source_target_pairs={{0,32},{32,0},{4,36},{36,4},{8,40},{40,8},{12,44},{44,12},{16,48},... | collective-permute-start | bytes 3145736 | tf_op jit(solution)/shard_map/ppermute | solution.py:21
  389.6 88.1 %collective-permute-start.5 = (f32[256,2,512]{2,0,1:T(8,128)}, f32[256,2,512]{2,0,1:T(8,128)}, u32[]{:S(2)}, u32[]{:S(2)}) collective-permute-start(f32[256,2,512]{2,0,1:T(8,128)} %get-tuple-element.88), channel_id=1, source_target_pairs={{0,32},{32,0},{4,36},{36,4},{8,40},{40,8},{12,44},{44,12},{16,48},... | collective-permute-start | bytes 3145736 | tf_op jit(solution)/shard_map/ppermute | solution.py:21
  483.8 24.5 %collective-permute-start.18 = (f32[256,2,512]{2,0,1:T(8,128)}, f32[256,2,512]{2,0,1:T(8,128)S(1)}, u32[]{:S(2)}, u32[]{:S(2)}) collective-permute-start(f32[256,2,512]{2,0,1:T(8,128)} %get-tuple-element.42), channel_id=1, source_target_pairs={{0,16},{16,0},{4,20},{20,4},{8,24},{24,8},{12,28},{28,12},{32,48},... | collective-permute-start | bytes 3145736 | tf_op jit(solution)/shard_map/ppermute | solution.py:21
  486.7 44.1 %collective-permute-start.19 = (f32[256,2,512]{2,0,1:T(8,128)}, f32[256,2,512]{2,0,1:T(8,128)S(1)}, u32[]{:S(2)}, u32[]{:S(2)}) collective-permute-start(f32[256,2,512]{2,0,1:T(8,128)} %get-tuple-element.43), channel_id=1, source_target_pairs={{0,16},{16,0},{4,20},{20,4},{8,24},{24,8},{12,28},{28,12},{32,48},... | collective-permute-start | bytes 3145736 | tf_op jit(solution)/shard_map/ppermute | solution.py:21
  486.9 66.4 %collective-permute-start.6 = (f32[256,2,512]{2,0,1:T(8,128)}, f32[256,2,512]{2,0,1:T(8,128)}, u32[]{:S(2)}, u32[]{:S(2)}) collective-permute-start(f32[256,2,512]{2,0,1:T(8,128)} %get-tuple-element.85), channel_id=1, source_target_pairs={{0,16},{16,0},{4,20},{20,4},{8,24},{24,8},{12,28},{28,12},{32,48},... | collective-permute-start | bytes 3145736 | tf_op jit(solution)/shard_map/ppermute | solution.py:21
  489.7 86.1 %collective-permute-start.7 = (f32[256,2,512]{2,0,1:T(8,128)}, f32[256,2,512]{2,0,1:T(8,128)}, u32[]{:S(2)}, u32[]{:S(2)}) collective-permute-start(f32[256,2,512]{2,0,1:T(8,128)} %get-tuple-element.86), channel_id=1, source_target_pairs={{0,16},{16,0},{4,20},{20,4},{8,24},{24,8},{12,28},{28,12},{32,48},... | collective-permute-start | bytes 3145736 | tf_op jit(solution)/shard_map/ppermute | solution.py:21
  508.3 67.5 %copy-start.3 = (f32[256,2,512]{2,0,1:T(8,128)}, f32[256,2,512]{2,0,1:T(8,128)S(1)}, u32[]{:S(2)}) copy-start(f32[256,2,512]{2,0,1:T(8,128)S(1)} %collective-permute-done.18) | copy-start | bytes 3145732
  530.8 45.1 %copy-start.5 = (f32[256,2,512]{2,0,1:T(8,128)}, f32[256,2,512]{2,0,1:T(8,128)S(1)}, u32[]{:S(2)}) copy-start(f32[256,2,512]{2,0,1:T(8,128)S(1)} %collective-permute-done.19) | copy-start | bytes 3145732
  582.0 21.9 %collective-permute-start.20 = (f32[256,2,512]{2,0,1:T(8,128)S(1)}, f32[256,2,512]{2,0,1:T(8,128)}, u32[]{:S(2)}, u32[]{:S(2)}) collective-permute-start(f32[256,2,512]{2,0,1:T(8,128)S(1)} %get-tuple-element.40), channel_id=1, source_target_pairs={{0,8},{8,0},{4,12},{12,4},{16,24},{24,16},{20,28},{28,20},{32,40},... | collective-permute-start | bytes 3145736 | tf_op jit(solution)/shard_map/ppermute | solution.py:21
  583.2 43.1 %collective-permute-start.21 = (f32[256,2,512]{2,0,1:T(8,128)S(1)}, f32[256,2,512]{2,0,1:T(8,128)}, u32[]{:S(2)}, u32[]{:S(2)}) collective-permute-start(f32[256,2,512]{2,0,1:T(8,128)S(1)} %get-tuple-element.41), channel_id=1, source_target_pairs={{0,8},{8,0},{4,12},{12,4},{16,24},{24,16},{20,28},{28,20},{32,40},... | collective-permute-start | bytes 3145736 | tf_op jit(solution)/shard_map/ppermute | solution.py:21
  583.5 65.4 %collective-permute-start.8 = (f32[256,2,512]{2,0,1:T(8,128)}, f32[256,2,512]{2,0,1:T(8,128)}, u32[]{:S(2)}, u32[]{:S(2)}) collective-permute-start(f32[256,2,512]{2,0,1:T(8,128)} %get-tuple-element.83), channel_id=1, source_target_pairs={{0,8},{8,0},{4,12},{12,4},{16,24},{24,16},{20,28},{28,20},{32,40},... | collective-permute-start | bytes 3145736 | tf_op jit(solution)/shard_map/ppermute | solution.py:21
  584.7 86.6 %collective-permute-start.9 = (f32[256,2,512]{2,0,1:T(8,128)}, f32[256,2,512]{2,0,1:T(8,128)}, u32[]{:S(2)}, u32[]{:S(2)}) collective-permute-start(f32[256,2,512]{2,0,1:T(8,128)} %get-tuple-element.84), channel_id=1, source_target_pairs={{0,8},{8,0},{4,12},{12,4},{16,24},{24,16},{20,28},{28,20},{32,40},... | collective-permute-start | bytes 3145736 | tf_op jit(solution)/shard_map/ppermute | solution.py:21
  677.4 6.3 collective-permute-start.10
  681.2 4.0 collective-permute-start.11
  681.2 5.6 collective-permute-start.22
  681.7 6.6 collective-permute-start.23
  763.2 7.3 collective-permute-start.24
  770.3 1.9 collective-permute-start.25
  776.3 13.5 %collective-permute-start.26 = (bf16[256,2,512]{2,0,1:T(8,128)(2,1)}, bf16[256,2,512]{2,0,1:T(8,128)(2,1)S(1)}, u32[]{:S(2)}, u32[]{:S(2)}) collective-permute-start(bf16[256,2,512]{2,0,1:T(8,128)(2,1)} %get-tuple-element.32), channel_id=1, source_target_pairs={{0,8},{8,0},{4,12},{12,4},{16,24},{24,16},{20,28},{28,20},{32,40},... | collective-permute-start | bytes 1572872 | tf_op jit(solution)/shard_map/ppermute | solution.py:21
  777.6 23.7 %collective-permute-start.27 = (bf16[256,2,512]{2,0,1:T(8,128)(2,1)}, bf16[256,2,512]{2,0,1:T(8,128)(2,1)}, u32[]{:S(2)}, u32[]{:S(2)}) collective-permute-start(bf16[256,2,512]{2,0,1:T(8,128)(2,1)} %get-tuple-element.70), channel_id=1, source_target_pairs={{0,8},{8,0},{4,12},{12,4},{16,24},{24,16},{20,28},{28,20},{32,40},... | collective-permute-start | bytes 1572872 | tf_op jit(solution)/shard_map/ppermute | solution.py:21
  789.9 11.3 %copy-start.9 = (bf16[256,2,512]{2,0,1:T(8,128)(2,1)}, bf16[256,2,512]{2,0,1:T(8,128)(2,1)S(1)}, u32[]{:S(2)}) copy-start(bf16[256,2,512]{2,0,1:T(8,128)(2,1)S(1)} %collective-permute-done.26) | copy-start | bytes 1572868
  804.4 14.2 %collective-permute-start.28 = (bf16[256,2,512]{2,0,1:T(8,128)(2,1)}, bf16[256,2,512]{2,0,1:T(8,128)(2,1)S(1)}, u32[]{:S(2)}, u32[]{:S(2)}) collective-permute-start(bf16[256,2,512]{2,0,1:T(8,128)(2,1)} %get-tuple-element.28), channel_id=1, source_target_pairs={{0,16},{16,0},{4,20},{20,4},{8,24},{24,8},{12,28},{28,12},{32,48},... | collective-permute-start | bytes 1572872 | tf_op jit(solution)/shard_map/ppermute | solution.py:21
  807.2 22.7 %collective-permute-start.29 = (bf16[256,2,512]{2,0,1:T(8,128)(2,1)S(1)}, bf16[256,2,512]{2,0,1:T(8,128)(2,1)S(1)}, u32[]{:S(2)}, u32[]{:S(2)}) collective-permute-start(bf16[256,2,512]{2,0,1:T(8,128)(2,1)S(1)} %get-tuple-element.68), channel_id=1, source_target_pairs={{0,16},{16,0},{4,20},{20,4},{8,24},{24,8},{12,28},{28,12},{32,48},... | collective-permute-start | bytes 1572872 | tf_op jit(solution)/shard_map/ppermute | solution.py:21
  818.6 11.2 copy-start.10
  833.9 13.7 %collective-permute-start.30 = (bf16[256,2,512]{2,0,1:T(8,128)(2,1)}, bf16[256,2,512]{2,0,1:T(8,128)(2,1)}, u32[]{:S(2)}, u32[]{:S(2)}) collective-permute-start(bf16[256,2,512]{2,0,1:T(8,128)(2,1)} %get-tuple-element.24), channel_id=1, source_target_pairs={{0,32},{32,0},{4,36},{36,4},{8,40},{40,8},{12,44},{44,12},{16,48},... | collective-permute-start | bytes 1572872 | tf_op jit(solution)/shard_map/ppermute | solution.py:21
  836.9 22.0 %collective-permute-start.31 = (bf16[256,2,512]{2,0,1:T(8,128)(2,1)S(1)}, bf16[256,2,512]{2,0,1:T(8,128)(2,1)}, u32[]{:S(2)}, u32[]{:S(2)}) collective-permute-start(bf16[256,2,512]{2,0,1:T(8,128)(2,1)S(1)} %get-tuple-element.66), channel_id=1, source_target_pairs={{0,32},{32,0},{4,36},{36,4},{8,40},{40,8},{12,44},{44,12},{16,48},... | collective-permute-start | bytes 1572872 | tf_op jit(solution)/shard_map/ppermute | solution.py:21
  862.1 37.9 %collective-permute-start.32 = (bf16[256,2,512]{2,0,1:T(8,128)(2,1)}, bf16[256,2,512]{2,0,1:T(8,128)(2,1)S(1)}, u32[]{:S(2)}, u32[]{:S(2)}) collective-permute-start(bf16[256,2,512]{2,0,1:T(8,128)(2,1)} %get-tuple-element.20), channel_id=1, source_target_pairs={{0,64},{64,0},{4,68},{68,4},{8,72},{72,8},{12,76},{76,12},{16,80},... | collective-permute-start | bytes 1572872 | tf_op jit(solution)/shard_map/ppermute | solution.py:21
  865.5 45.7 %collective-permute-start.33 = (bf16[256,2,512]{2,0,1:T(8,128)(2,1)S(1)}, bf16[256,2,512]{2,0,1:T(8,128)(2,1)S(1)}, u32[]{:S(2)}, u32[]{:S(2)}) collective-permute-start(bf16[256,2,512]{2,0,1:T(8,128)(2,1)S(1)} %get-tuple-element.64), channel_id=1, source_target_pairs={{0,64},{64,0},{4,68},{68,4},{8,72},{72,8},{12,76},{76,12},{16,80},... | collective-permute-start | bytes 1572872 | tf_op jit(solution)/shard_map/ppermute | solution.py:21
  900.0 11.2 copy-start.7
  915.5 50.8 %collective-permute-start.34 = (bf16[256,2,512]{2,0,1:T(8,128)(2,1)}, bf16[256,2,512]{2,0,1:T(8,128)(2,1)}, u32[]{:S(2)}, u32[]{:S(2)}) collective-permute-start(bf16[256,2,512]{2,0,1:T(8,128)(2,1)} %get-tuple-element.16), channel_id=1, source_target_pairs={{0,128},{128,0},{4,132},{132,4},{8,136},{136,8},{12,140},{140,12},... | collective-permute-start | bytes 1572872 | tf_op jit(solution)/shard_map/ppermute | solution.py:21
  920.7 45.4 %collective-permute-start.35 = (bf16[256,2,512]{2,0,1:T(8,128)(2,1)}, bf16[256,2,512]{2,0,1:T(8,128)(2,1)S(1)}, u32[]{:S(2)}, u32[]{:S(2)}) collective-permute-start(bf16[256,2,512]{2,0,1:T(8,128)(2,1)} %get-tuple-element.62), channel_id=1, source_target_pairs={{0,128},{128,0},{4,132},{132,4},{8,136},{136,8},{12,140},{140,12},... | collective-permute-start | bytes 1572872 | tf_op jit(solution)/shard_map/ppermute | solution.py:21
  968.2 11.0 copy-start.14
  969.0 9.8 all-to-all-start
  1052.1 57.0 %all-to-all-start.2 = ((bf16[64,16,1024]{2,1,0:T(8,128)(2,1)}), bf16[64,16,1024]{2,1,0:T(8,128)(2,1)S(1)}, u32[]{:S(2)}, u32[]{:S(2)}) async-start(bf16[64,16,1024]{2,1,0:T(8,128)(2,1)} %convolution_convert_fusion), calls=%async_computation.2 | async-start | bytes 4194304 | tf_op jit(solution)/shard_map/all_to_all | solution.py:166
  1122.3 8.9 all-to-all-start.3
  (9 other events, 37.0 us)
where the time goes:
time: 1140 us; the launch traced here: 1130 us
  waiting for transfers between devices  803 us (70%)
  starting transfers between devices  94.8 us (8%)
  matrix products  83.3 us (7%)
  other arithmetic  63.7 us (6%)
  blocking collectives  60.6 us (5%)
  local copies, waits for them, and re-layouts  25.2 us (2%)
    ppermute x36, waiting for transfers between devices, partner(): return lax.ppermute(block, axis, route)  744 us
    ppermute x36, starting transfers between devices, partner(): return lax.ppermute(block, axis, route)  79.6 us
    all_to_all x1, blocking collectives, body(): lax.all_to_all(send_rows.reshape(shards, parts_dev * CAP, width), 'ctx',...  60.6 us
    all_to_all x1, waiting for transfers between devices, body(): lax.all_to_all(result.reshape(shards, parts_dev * CAP, width), 'ctx', spl...  49 us
    select_n x6, other arithmetic, forward_pair(): jnp.where(upper, diff_real, own_real + far_real)  33.7 us
  transfers between devices with their start and end apart: 39, of which 37 were waited for; matrix products, arithmetic and copies ran while one was open for 1% of the time, Pallas kernels for 0%

commit v1 on v0

v1 whole, which is shorter than its diff:
```python
import math

import jax
import jax.numpy as jnp
import numpy as np
from jax import lax
from jax.experimental import pallas as pl
from jax.experimental.pallas import tpu as pltpu
from jax.sharding import PartitionSpec as P

CAP = 16
bf16 = jnp.bfloat16
f32 = jnp.float32


def dft_constants(shards, tok, chans):
    total = shards * tok
    fields = 2 * chans
    row = np.arange(shards)
    col = np.arange(tok)
    outer = 2.0 * np.pi * row[None, :] * (row[:, None] + 0.25) / shards
    first = np.concatenate([np.cos(outer), -np.sin(outer)], axis=0)
    first = np.repeat(first, fields, axis=1)
    last = np.concatenate([np.cos(outer.T), -np.sin(outer.T)], axis=1) / total
    last = np.repeat(last, chans, axis=0)
    turn = 2.0 * np.pi * (row[:, None] + 0.25) * col[None, :] / total
    inner = 2.0 * np.pi * ((col[:, None] * col[None, :]) % tok) / tok
    as16 = lambda a: jnp.asarray(a.astype(np.float32), bf16)
    as32 = lambda a: jnp.asarray(a.astype(np.float32))
    return (
        as16(first),
        as32(np.cos(turn)),
        as32(-np.sin(turn)),
        as16(np.cos(inner)),
        as16(np.sin(inner)),
        as16(last),
    )


def dot(a, b):
    return jnp.dot(a, b, preferred_element_type=f32)


def conv_kernel(shards, chans, r_ref, first_ref, tr_ref, ti_ref, c_ref, s_ref, last_ref, o_ref, re_ref, im_ref):
    fields = 2 * chans
    data = r_ref[...]
    first = first_ref[...]
    lane = lax.broadcasted_iota(jnp.int32, first.shape, 1) % fields
    tr, ti = tr_ref[...], ti_ref[...]
    for field in range(fields):
        g = dot(jnp.where(lane == field, first, jnp.zeros_like(first)), data)
        g_re, g_im = g[:shards], g[shards:]
        rows = pl.ds(field * shards, shards)
        re_ref[rows, :] = (g_re * tr - g_im * ti).astype(bf16)
        im_ref[rows, :] = (g_re * ti + g_im * tr).astype(bf16)
    cos, sin = c_ref[...], s_ref[...]
    re, im = re_ref[...], im_ref[...]
    x_re = dot(re, cos) + dot(im, sin)
    x_im = dot(im, cos) - dot(re, sin)
    half = chans * shards
    p_re = (x_re[:half] * x_re[half:] - x_im[:half] * x_im[half:]).astype(bf16)
    p_im = (x_re[:half] * x_im[half:] + x_im[:half] * x_re[half:]).astype(bf16)
    g_re = dot(p_re, cos) - dot(p_im, sin)
    g_im = dot(p_im, cos) + dot(p_re, sin)
    last = last_ref[...]
    row = lax.broadcasted_iota(jnp.int32, last.shape, 0) % chans
    total = jnp.zeros(o_ref.shape, f32)
    for chan in range(chans):
        rows = slice(chan * shards, (chan + 1) * shards)
        a = (g_re[rows] * tr + g_im[rows] * ti).astype(bf16)
        b = (g_im[rows] * tr - g_re[rows] * ti).astype(bf16)
        both = jnp.concatenate([a, b], axis=0)
        total += dot(jnp.where(row == chan, last, jnp.zeros_like(last)), both)
    o_ref[...] = total.astype(bf16)


def route_kernel(experts, x_ref, gain_ref, router_ref, routes_ref, routes_t_ref, send_ref, hi_ref, lo_ref):
    count = x_ref.shape[0]
    slots = experts * CAP
    x = x_ref[...].astype(f32)
    scale = lax.rsqrt(jnp.mean(x * x, axis=-1, keepdims=True) + 1e-05)
    normed = (x * scale * gain_ref[...]).astype(bf16)
    logits = jnp.dot(
        normed.astype(f32), router_ref[...], precision=lax.Precision.HIGHEST, preferred_element_type=f32
    )
    gates = jax.nn.sigmoid(logits)
    g_hi = gates.astype(bf16)
    g_lo = (gates - g_hi.astype(f32)).astype(bf16)
    ids = lax.broadcasted_iota(jnp.int32, (count, experts), 1)
    routes = routes_ref[...]
    named = ((routes[:, 0:1] == ids) | (routes[:, 1:2] == ids)).astype(f32).astype(bf16)
    rows = lax.broadcasted_iota(jnp.int32, (count, count), 0)
    cols = lax.broadcasted_iota(jnp.int32, (count, count), 1)
    rank = dot((cols < rows).astype(f32).astype(bf16), named).astype(bf16)
    spread = (
        lax.broadcasted_iota(jnp.int32, (experts, slots), 1) // CAP
        == lax.broadcasted_iota(jnp.int32, (experts, slots), 0)
    ).astype(f32).astype(bf16)
    slot = (lax.broadcasted_iota(jnp.int32, (count, slots), 1) % CAP).astype(f32)
    here = (dot(named, spread) > 0.5) & (dot(rank, spread) == slot)
    hi_ref[...] = jnp.where(here, dot(g_hi, spread), 0.0).astype(bf16)
    lo_ref[...] = jnp.where(here, dot(g_lo, spread), 0.0).astype(bf16)
    ids_t = lax.broadcasted_iota(jnp.int32, (experts, count), 0)
    routes_t = routes_t_ref[...]
    named_t = ((routes_t[0:1, :] == ids_t) | (routes_t[1:2, :] == ids_t)).astype(f32).astype(bf16)
    rank_t = dot(named_t, (rows < cols).astype(f32).astype(bf16)).astype(bf16)
    spread_t = (
        lax.broadcasted_iota(jnp.int32, (slots, experts), 0) // CAP
        == lax.broadcasted_iota(jnp.int32, (slots, experts), 1)
    ).astype(f32).astype(bf16)
    slot_t = (lax.broadcasted_iota(jnp.int32, (slots, count), 0) % CAP).astype(f32)
    here_t = (dot(spread_t, named_t) > 0.5) & (dot(spread_t, rank_t) == slot_t)
    send_ref[...] = dot(here_t.astype(f32).astype(bf16), normed).astype(bf16)


def expert_kernel(x_ref, up_ref, down_ref, o_ref):
    hidden = jax.nn.gelu(dot(x_ref[...], up_ref[...]), approximate=True).astype(bf16)
    o_ref[...] = dot(hidden, down_ref[...]).astype(bf16)


def combine_kernel(hi_ref, lo_ref, back_ref, o_ref):
    back = back_ref[...]
    o_ref[...] = (dot(hi_ref[...], back) + dot(lo_ref[...], back)).astype(bf16)


def call(kernel, out_shape, *args, scratch=()):
    return pl.pallas_call(
        kernel,
        out_shape=out_shape,
        in_specs=[pl.BlockSpec(memory_space=pltpu.VMEM)] * len(args),
        out_specs=jax.tree.map(lambda _: pl.BlockSpec(memory_space=pltpu.VMEM), out_shape),
        scratch_shapes=list(scratch),
    )(*args)


def body(signal, gate_v, taps, skip, norm_gain, router, w_up, w_down, routes):
    tok_dev, ch_dev = signal.shape
    shards = lax.axis_size("ctx")
    chans = ch_dev // shards
    experts = router.shape[1]
    width = norm_gain.shape[0]
    shape = jax.ShapeDtypeStruct
    constants = dft_constants(shards, tok_dev, chans)

    sig_t = signal.T.reshape(shards, chans, tok_dev)
    tap_t = taps.astype(bf16).T.reshape(shards, chans, tok_dev)
    packed = jnp.concatenate([sig_t, tap_t], axis=1)
    fields = lax.all_to_all(packed, "ctx", split_axis=0, concat_axis=0, tiled=True)
    conv = call(
        lambda *refs: conv_kernel(shards, chans, *refs),
        shape((shards * chans, tok_dev), bf16),
        fields.reshape(shards * 2 * chans, tok_dev),
        *constants,
        scratch=[pltpu.VMEM((2 * chans * shards, tok_dev), bf16)] * 2,
    )
    conv = lax.all_to_all(
        conv.reshape(shards, chans, tok_dev), "ctx", split_axis=0, concat_axis=0, tiled=True
    )
    conv = conv.reshape(ch_dev, tok_dev).T.astype(f32)
    mixed = (gate_v.astype(f32) * (conv + skip * signal.astype(f32))).astype(bf16)
    full_rows = lax.all_to_all(mixed, "ch", split_axis=0, concat_axis=1, tiled=True)
    slots = experts * CAP
    rows = full_rows.shape[0]
    send, hi, lo = call(
        lambda *refs: route_kernel(experts, *refs),
        (shape((slots, width), bf16), shape((rows, slots), bf16), shape((rows, slots), bf16)),
        full_rows,
        norm_gain[None, :],
        router,
        routes,
        routes.T,
    )
    same_side = [[2 * e + side for e in range(shards // 2)] for side in range(2)]
    swap = [(i, i ^ 1) for i in range(shards)]

    def exchange(block):
        out = lax.all_to_all(
            block.reshape(experts, CAP, width),
            "ctx",
            split_axis=0,
            concat_axis=0,
            axis_index_groups=same_side,
            tiled=True,
        )
        return out.reshape(slots, width)

    mine = exchange(send)
    theirs = lax.ppermute(mine, "ctx", swap)
    up, down = w_up[0], w_down[0]
    out_theirs = call(expert_kernel, shape((slots, width), bf16), theirs, up, down)
    partner_part = lax.ppermute(out_theirs, "ctx", swap)
    out_mine = call(expert_kernel, shape((slots, width), bf16), mine, up, down)
    summed = (out_mine.astype(f32) + partner_part.astype(f32)).astype(bf16)
    back = exchange(summed)
    moe_rows = call(combine_kernel, shape((rows, width), bf16), hi, lo, back)
    moe_out = lax.all_to_all(moe_rows, "ch", split_axis=1, concat_axis=0, tiled=True)
    return (mixed, moe_out)


def solution(mesh):
    in_specs = (
        P("ctx", "ch"),
        P("ctx", "ch"),
        P("ctx", "ch"),
        P("ch"),
        P(),
        P(),
        P("ctx", None, None),
        P("ctx", None, None),
        P(("ctx", "ch"), None),
    )
    out_specs = (P("ctx", "ch"), P("ctx", "ch"))
    return jax.shard_map(body, mesh=mesh, in_specs=in_specs, out_specs=out_specs, check_vma=False)
```

time: 1140 us -> 167 us (0.15)
  waiting for transfers between devices: 803 us -> 19.2 us
  matrix products: 83.3 us -> 0 us
  starting transfers between devices: 94.8 us -> 13.8 us
  other arithmetic: 63.7 us -> 3.15 us
  blocking collectives: 60.6 us -> 100 us
  Pallas kernels: 0 us -> 18.9 us
  local copies, waits for them, and re-layouts: 25.2 us -> 8.5 us
    ppermute x36 -> x2, waiting for transfers between devices: 744 us -> 2.29 us  [the longest x1 2.29 us: body(): theirs = lax.ppermute(mine, 'ctx', swap)]
    dot_general x14 -> x0, matrix products: 83.3 us -> none  [the longest x2 13 us: local_forward(): jnp.matmul(imag_part, cosine, precision=precise)]
    ppermute x36 -> x2, starting transfers between devices: 79.6 us -> 3.97 us  [the longest x1 3.59 us: body(): theirs = lax.ppermute(mine, 'ctx', swap)]
    all_to_all x2 -> x1, waiting for transfers between devices: 53.7 us -> 12.8 us  [body(): lax.all_to_all(conv.reshape(shards, chans, tok_dev), 'ctx', split_axis=0,...]
    all_to_all x1 -> x4, blocking collectives: 60.6 us -> 100 us  [the longest x2 61.7 us: exchange(): lax.all_to_all(block.reshape(experts, CAP, width), 'ctx', split_axis=0, c...]
    select_n x8 -> x0, other arithmetic: 33.7 us -> none  [the longest x6 33.7 us: forward_pair(): jnp.where(upper, diff_real, own_real + far_real)]
    pallas_call x0 -> x5, Pallas kernels: none -> 18.9 us  [call(): pl.pallas_call(kernel, out_shape=out_shape, in_specs=[pl.BlockSpec(memory...]
    convert_element_type x10 -> x2, other arithmetic: 17.1 us -> 1.78 us  [the longest x1 1.61 us: body(): summed = (out_mine.astype(f32) + partner_part.astype(f32)).astype(bf16)]
  transfers between devices with their start and end apart: 39 -> 4, of which waited for: 37 -> 3; matrix products, arithmetic and copies ran while one was open for 1% -> 1% of each run, Pallas kernels for 0% -> 2%
where the time goes in v1:
time: 167 us; the launch traced here: 165 us
  blocking collectives  100 us (60%)
  waiting for transfers between devices  19.2 us (11%)
  Pallas kernels  18.9 us (11%)
  starting transfers between devices  13.8 us (8%)
  local copies, waits for them, and re-layouts  8.5 us (5%)
  other arithmetic  3.15 us (2%)
    all_to_all x2, blocking collectives, exchange(): lax.all_to_all(block.reshape(experts, CAP, width), 'ctx', split_axis=0, c...  61.7 us
    all_to_all x1, blocking collectives, body(): lax.all_to_all(packed, 'ctx', split_axis=0, concat_axis=0, tiled=True)  30.6 us
    pallas_call x5, Pallas kernels, call(): pl.pallas_call(kernel, out_shape=out_shape, in_specs=[pl.BlockSpec(memory...  18.9 us
    all_to_all x1, waiting for transfers between devices, body(): lax.all_to_all(conv.reshape(shards, chans, tok_dev), 'ctx', split_axis=0,...  12.8 us
    all_to_all x1, blocking collectives, body(): lax.all_to_all(moe_rows, 'ch', split_axis=1, concat_axis=0, tiled=True)  7.92 us
    all_to_all x1, starting transfers between devices, body(): lax.all_to_all(conv.reshape(shards, chans, tok_dev), 'ctx', split_axis=0,...  5.69 us
    unnamed x20, local copies, waits for them, and re-layouts  4.59 us
    all_to_all x1, starting transfers between devices, body(): lax.all_to_all(mixed, 'ch', split_axis=0, concat_axis=1, tiled=True)  4.18 us
  transfers between devices with their start and end apart: 4, of which 3 were waited for; matrix products, arithmetic and copies ran while one was open for 1% of the time, Pallas kernels for 2%

profile of v1, /device:TPU:1, one launch (start us, length us, event | category | flops | bytes accessed | tf_op | source)
XLA Modules:
  0.0 164.5 jit_solution(6674653344885326127)
XLA Ops:
  0.6 0.0 copy-start.2
  0.6 1.1 convert_bitcast_fusion
  1.8 0.1 copy.35
  1.9 0.1 reshape.39
  2.0 0.0 copy-done.2
  2.0 0.1 copy.34
  2.1 0.1 reshape.38
  2.2 0.3 pad_maximum_fusion
  2.5 30.6 %all_to_all.58 = bf16[64,8,512]{2,1,0:T(8,128)(2,1)} all-to-all(bf16[64,8,512]{2,1,0:T(8,128)(2,1)S(1)} %pad_maximum_fusion), channel_id=1, replica_groups=mesh['ctx'=64,'ch'=4] {'ctx'}, dimensions={0} | all-to-all | bytes 1048576 | tf_op jit(solution)/shard_map/all_to_all | solution.py:148
  33.0 5.3 %shard_map.158 = bf16[256,512]{1,0:T(8,128)(2,1)} custom-call(bf16[512,512]{1,0:T(8,128)(2,1)} %bitcast.33, bf16[128,512]{1,0:T(8,128)(2,1)} %constant.12.clone.refs_1_, f32[64,512]{1,0:T(8,128)} %constant.13.clone.refs_2_, f32[64,512]{1,0:T(8,128)} %constant.14.clone.refs_3_, bf16[512,512]{1,0:T(8,128)(2,1)} %constant.15.clone.refs_4_, ...), custom_call_target="tpu_custom_call" | custom-call | tf_op jit(solution)/shard_map/pallas_call | solution.py:127
  38.3 0.0 copy-start.3
  38.3 1.8 %reshape.41 = bf16[64,4,512]{2,1,0:T(4,128)(2,1)} reshape(bf16[256,512]{1,0:T(8,128)(2,1)} %shard_map.158) | data formatting | bytes 524288 | tf_op jit(solution)/shard_map/reshape | solution.py:157
  40.1 5.7 %all-to-all-start.1 = ((bf16[64,4,512]{2,1,0:T(4,128)(2,1)}), bf16[64,4,512]{2,1,0:T(4,128)(2,1)S(1)}, u32[]{:S(2)}, u32[]{:S(2)}) async-start(bf16[64,4,512]{2,1,0:T(4,128)(2,1)} %reshape.41), calls=%async_computation.1 | async-start | bytes 524288 | tf_op jit(solution)/shard_map/all_to_all | solution.py:156
  45.8 0.0 copy-start.6
  45.8 0.1 copy.36
  45.9 0.0 copy-done.3
  45.9 0.1 copy.33
  46.1 12.8 %all-to-all-done.1 = bf16[64,4,512]{2,1,0:T(4,128)(2,1)S(1)} async-done(((bf16[64,4,512]{2,1,0:T(4,128)(2,1)}), bf16[64,4,512]{2,1,0:T(4,128)(2,1)S(1)}, u32[]{:S(2)}, u32[]{:S(2)}) %all-to-all-start.1) | async-done | bytes 262176 | tf_op jit(solution)/shard_map/all_to_all | solution.py:156
  58.9 0.0 copy-done.6
  58.9 0.0 copy-start.5
  58.9 0.0 copy-start.4
  58.9 0.2 fusion.1
  59.1 0.8 copy.42
  59.9 4.2 %all-to-all-start.2 = ((bf16[4,128,256]{2,1,0:T(8,128)(2,1)}), bf16[4,128,256]{2,1,0:T(8,128)(2,1)S(1)}, u32[]{:S(2)}, u32[]{:S(2)}) async-start(bf16[4,128,256]{2,1,0:T(8,128)(2,1)} %bitcast.4), calls=%async_computation.2 | async-start | bytes 524288 | tf_op jit(solution)/shard_map/all_to_all | solution.py:161
  64.1 0.0 copy-done.5
  64.1 0.7 copy.40.refs_3_
  64.9 0.0 copy-done.4
  64.9 1.0 copy.39.refs_2_
  65.9 4.2 %all-to-all-done.2 = bf16[4,128,256]{2,1,0:T(8,128)(2,1)S(1)} async-done(((bf16[4,128,256]{2,1,0:T(8,128)(2,1)}), bf16[4,128,256]{2,1,0:T(8,128)(2,1)S(1)}, u32[]{:S(2)}, u32[]{:S(2)}) %all-to-all-start.2) | async-done | bytes 262176 | tf_op jit(solution)/shard_map/all_to_all | solution.py:161
  70.0 0.7 copy.45
  70.8 3.6 %shard_map.159 = (bf16[512,1024]{1,0:T(8,128)(2,1)}, bf16[128,512]{1,0:T(8,128)(2,1)}, bf16[128,512]{1,0:T(8,128)(2,1)}) custom-call(bf16[128,1024]{1,0:T(8,128)(2,1)} %bitcast.43, f32[1,1024]{1,0:T(1,128)} %bitcast.45, f32[1024,32]{1,0:T(8,128)} %copy.39.refs_2_, s32[128,2]{1,0:T(8,128)} %copy.40.refs_3_, s32[2,128]{1,0:T(2,128)} %bitcast.46), custom_call_target="tpu_custom_call" | custom-call | tf_op jit(solution)/shard_map/pallas_call | solution.py:127
  74.4 29.6 %all_to_all.59 = bf16[32,16,1024]{2,1,0:T(8,128)(2,1)S(1)} all-to-all(bf16[32,16,1024]{2,1,0:T(8,128)(2,1)} %bitcast.38), channel_id=1, replica_groups={{0,8,16,24,32,40,48,56,64,72,80,88,96,104,112,120,128,136,144,152,160,1..., dimensions={0} | all-to-all | bytes 2097152 | tf_op jit(solution)/shard_map/all_to_all | solution.py:177
  104.0 0.0 copy-start
  104.0 3.6 %collective-permute-start = (bf16[512,1024]{1,0:T(8,128)(2,1)S(1)}, bf16[512,1024]{1,0:T(8,128)(2,1)S(1)}, u32[]{:S(2)}, u32[]{:S(2)}) collective-permute-start(bf16[512,1024]{1,0:T(8,128)(2,1)S(1)} %bitcast.29), channel_id=1, source_target_pairs={{0,4},{4,0},{8,12},{12,8},{16,20},{20,16},{24,28},{28,24},{32,36},... | collective-permute-start | bytes 3145736 | tf_op jit(solution)/shard_map/ppermute | solution.py:188
  107.6 2.3 %collective-permute-done.x_ref = bf16[512,1024]{1,0:T(8,128)(2,1)S(1)} collective-permute-done((bf16[512,1024]{1,0:T(8,128)(2,1)S(1)}, bf16[512,1024]{1,0:T(8,128)(2,1)S(1)}, u32[]{:S(2)}, u32[]{:S(2)}) %collective-permute-start) | collective-permute-done | bytes 1048608 | tf_op jit(solution)/shard_map/ppermute | solution.py:188
  109.9 0.0 copy-start.1
  109.9 1.0 copy-done.1
  110.9 3.8 %shard_map.161 = bf16[512,1024]{1,0:T(8,128)(2,1)} custom-call(bf16[512,1024]{1,0:T(8,128)(2,1)} %copy-done.1, bf16[1024,256]{1,0:T(8,128)(2,1)} %bitcast.34, bf16[256,1024]{1,0:T(8,128)(2,1)} %bitcast.36), custom_call_target="tpu_custom_call" | custom-call | tf_op jit(solution)/shard_map/pallas_call | solution.py:127
  114.7 0.0 copy-done
  114.7 0.4 collective-permute-start.1
  115.0 3.7 %shard_map.160 = bf16[512,1024]{1,0:T(8,128)(2,1)} custom-call(bf16[512,1024]{1,0:T(8,128)(2,1)} %bitcast.30, bf16[1024,256]{1,0:T(8,128)(2,1)} %bitcast.35, bf16[256,1024]{1,0:T(8,128)(2,1)} %bitcast.37), custom_call_target="tpu_custom_call" | custom-call | tf_op jit(solution)/shard_map/pallas_call | solution.py:127
  118.8 0.0 collective-permute-done.1
  118.8 1.6 add_convert_fusion
  120.4 32.0 %all_to_all.60 = bf16[32,16,1024]{2,1,0:T(8,128)(2,1)} all-to-all(bf16[32,16,1024]{2,1,0:T(8,128)(2,1)S(1)} %bitcast.31), channel_id=1, replica_groups={{0,8,16,24,32,40,48,56,64,72,80,88,96,104,112,120,128,136,144,152,160,1..., dimensions={0} | all-to-all | bytes 2097152 | tf_op jit(solution)/shard_map/all_to_all | solution.py:177
  152.4 2.5 %shard_map.162 = bf16[128,1024]{1,0:T(8,128)(2,1)} custom-call(bf16[128,512]{1,0:T(8,128)(2,1)} %get-tuple-element.5.hi_ref, bf16[128,512]{1,0:T(8,128)(2,1)} %get-tuple-element.6.lo_ref, bf16[512,1024]{1,0:T(8,128)(2,1)} %bitcast.32), custom_call_target="tpu_custom_call" | custom-call | tf_op jit(solution)/shard_map/pallas_call | solution.py:127
  154.9 1.0 copy.47
  155.9 7.9 %all_to_all.61 = bf16[128,4,256]{2,0,1:T(8,128)(2,1)S(1)} all-to-all(bf16[128,4,256]{2,0,1:T(8,128)(2,1)S(1)} %bitcast.41), channel_id=1, replica_groups=mesh['ctx'=64,'ch'=4] {'ch'}, dimensions={1} | all-to-all | bytes 524288 | tf_op jit(solution)/shard_map/all_to_all | solution.py:196
  163.8 0.7 copy.49
  (1 shorter events, 0.0 us)
Async XLA Ops:
  0.6 1.3 copy-start.2
  38.3 7.6 %copy-start.3 = (bf16[512,256]{1,0:T(8,128)(2,1)S(1)}, bf16[512,256]{1,0:T(8,128)(2,1)}, u32[]{:S(2)}) copy-start(bf16[512,256]{1,0:T(8,128)(2,1)} %param.16) | copy-start | bytes 786436
  40.1 18.8 %all-to-all-start.1 = ((bf16[64,4,512]{2,1,0:T(4,128)(2,1)}), bf16[64,4,512]{2,1,0:T(4,128)(2,1)S(1)}, u32[]{:S(2)}, u32[]{:S(2)}) async-start(bf16[64,4,512]{2,1,0:T(4,128)(2,1)} %reshape.41), calls=%async_computation.1 | async-start | bytes 524288 | tf_op jit(solution)/shard_map/all_to_all | solution.py:156
  45.8 13.1 %copy-start.6 = (f32[256]{0:T(256)S(1)}, f32[256]{0:T(256)}, u32[]{:S(2)}) copy-start(f32[256]{0:T(256)} %param.18) | copy-start | bytes 3076
  58.9 5.2 %copy-start.5 = (s32[128,2]{0,1:T(2,128)S(1)}, s32[128,2]{0,1:T(2,128)}, u32[]{:S(2)}) copy-start(s32[128,2]{0,1:T(2,128)} %param.23) | copy-start | bytes 3076
  58.9 5.9 %copy-start.4 = (f32[1024,32]{0,1:T(8,128)S(1)}, f32[1024,32]{0,1:T(8,128)}, u32[]{:S(2)}) copy-start(f32[1024,32]{0,1:T(8,128)} %param.20) | copy-start | bytes 393220
  59.9 10.1 %all-to-all-start.2 = ((bf16[4,128,256]{2,1,0:T(8,128)(2,1)}), bf16[4,128,256]{2,1,0:T(8,128)(2,1)S(1)}, u32[]{:S(2)}, u32[]{:S(2)}) async-start(bf16[4,128,256]{2,1,0:T(8,128)(2,1)} %bitcast.4), calls=%async_computation.2 | async-start | bytes 524288 | tf_op jit(solution)/shard_map/all_to_all | solution.py:161
  104.0 10.6 %copy-start = (bf16[32,16,1024]{2,1,0:T(8,128)(2,1)}, bf16[32,16,1024]{2,1,0:T(8,128)(2,1)S(1)}, u32[]{:S(2)}) copy-start(bf16[32,16,1024]{2,1,0:T(8,128)(2,1)S(1)} %all_to_all.59) | copy-start | bytes 3145732
  104.0 5.9 %collective-permute-start = (bf16[512,1024]{1,0:T(8,128)(2,1)S(1)}, bf16[512,1024]{1,0:T(8,128)(2,1)S(1)}, u32[]{:S(2)}, u32[]{:S(2)}) collective-permute-start(bf16[512,1024]{1,0:T(8,128)(2,1)S(1)} %bitcast.29), channel_id=1, source_target_pairs={{0,4},{4,0},{8,12},{12,8},{16,20},{20,16},{24,28},{28,24},{32,36},... | collective-permute-start | bytes 3145736 | tf_op jit(solution)/shard_map/ppermute | solution.py:188
  109.9 1.0 copy-start.1
  114.7 4.1 %collective-permute-start.1 = (bf16[512,1024]{1,0:T(8,128)(2,1)}, bf16[512,1024]{1,0:T(8,128)(2,1)S(1)}, u32[]{:S(2)}, u32[]{:S(2)}) collective-permute-start(bf16[512,1024]{1,0:T(8,128)(2,1)} %shard_map.161), channel_id=1, source_target_pairs={{0,4},{4,0},{8,12},{12,8},{16,20},{20,16},{24,28},{28,24},{32,36},... | collective-permute-start | bytes 3145736 | tf_op jit(solution)/shard_map/ppermute | solution.py:191

commit v2 on v1

--- a/solution.py
+++ b/solution.py
@@ -113,14 +113,136 @@
     send_ref[...] = dot(here_t.astype(f32).astype(bf16), normed).astype(bf16)
 
 
-def expert_kernel(x_ref, up_ref, down_ref, o_ref):
-    hidden = jax.nn.gelu(dot(x_ref[...], up_ref[...]), approximate=True).astype(bf16)
-    o_ref[...] = dot(hidden, down_ref[...]).astype(bf16)
-
-
-def combine_kernel(hi_ref, lo_ref, back_ref, o_ref):
-    back = back_ref[...]
-    o_ref[...] = (dot(hi_ref[...], back) + dot(lo_ref[...], back)).astype(bf16)
+def remote(src, dst, send_sem, recv_sem, **where):
+    return pltpu.make_async_remote_copy(
+        src_ref=src,
+        dst_ref=dst,
+        send_sem=send_sem,
+        recv_sem=recv_sem,
+        device_id=where,
+        device_id_type=pl.DeviceIdType.MESH,
+    )
+
+
+class Place:
+    def __init__(self, zs=8, xs=4):
+        self.zs, self.xs = zs, xs
+        self.me = lax.axis_index("ctx")
+        self.y = lax.axis_index("ch")
+        self.core = self.me % 2
+        self.chip = self.me // 2
+        self.z = self.chip // xs
+        self.x = self.chip % xs
+        self.twin = self.me + 1 - 2 * self.core
+
+    def at(self, dz, dx):
+        return (self.z + dz + self.zs) % self.zs * self.xs + (self.x + dx + self.xs) % self.xs
+
+
+def greet(place, zs, xs, ys):
+    barrier = pltpu.get_barrier_semaphore()
+
+    def tell(**where):
+        pl.semaphore_signal(barrier, inc=1, device_id=where, device_id_type=pl.DeviceIdType.MESH)
+
+    def chip(i, carry):
+        tell(ctx=place.at(i // xs, i % xs) * 2 + place.core)
+        return carry
+
+    lax.fori_loop(1, zs * xs, chip, 0)
+    tell(ctx=place.twin)
+    for dy in range(1, ys):
+        tell(ch=(place.y + dy) % ys)
+    pl.semaphore_wait(barrier, zs * xs - 1 + 1 + ys - 1)
+
+
+def offsets(q, half, j):
+    if half == 0:
+        return 4 - q, j
+    return (4 + q if q else 0), (j + 1) % 4
+
+
+def each(q, act):
+    for half in range(2):
+
+        def one(j, carry):
+            dz, dx = offsets(q, half, j)
+            act(q * 8 + half * 4 + j, dz, dx)
+            return carry
+
+        lax.fori_loop(0, 3 if q == 0 and half == 1 else 4, one, 0)
+
+
+def experts_kernel(
+    send, hi, lo, up_ref, down_ref, out, got, twin_got, part, twin_part, summed, back, moe, landed, own,
+    send_sem, got_sem, fs_sem, fr_sem, ps_sem, pr_sem, rs_sem, back_sem, ms_sem, mr_sem, local_sem,
+):
+    place = Place()
+    me, core, chip, y = place.me, place.core, place.chip, place.y
+    chunk = 8
+    rows = chunk * CAP
+    greet(place, 8, 4, 4)
+    for q in range(4):
+
+        def dispatch(slot, dz, dx):
+            to = place.at(dz, dx)
+            remote(send.at[to], got.at[slot], send_sem, got_sem.at[q], ctx=to * 2 + core).start()
+
+        each(q, dispatch)
+    keep = pltpu.make_async_copy(send.at[chip], got.at[7], local_sem.at[0])
+    keep.start()
+    keep_back = pltpu.make_async_copy(summed.at[7], back.at[chip], local_sem.at[1])
+
+    def mlp(block):
+        x = block.reshape(rows, block.shape[-1])
+        hidden = jax.nn.gelu(dot(x, up_ref[...]), approximate=True).astype(bf16)
+        return dot(hidden, down_ref[...])
+
+    for q in range(4):
+        slots = pl.ds(q * chunk, chunk)
+        here = pl.ds(q * chunk, 7) if q == 0 else slots
+        remote(send.at[here], got.at[here], send_sem, got_sem.at[q], ctx=me).wait_recv()
+        if q == 0:
+            keep.wait()
+        share = remote(got.at[slots], twin_got.at[slots], fs_sem.at[q], fr_sem.at[q], ctx=place.twin)
+        share.start()
+        own[...] = mlp(got[slots])
+        share.wait_recv()
+        part[slots] = mlp(twin_got[slots]).astype(bf16).reshape(chunk, CAP, -1)
+        give = remote(part.at[slots], twin_part.at[slots], ps_sem.at[q], pr_sem.at[q], ctx=place.twin)
+        give.start()
+        give.wait_recv()
+        total = own[...].reshape(chunk, CAP, -1) + twin_part[slots].astype(f32)
+        summed[slots] = total.astype(bf16)
+
+        def give_back(slot, dz, dx):
+            to = place.at(-dz, -dx)
+            remote(summed.at[slot], back.at[chip], rs_sem, back_sem, ctx=to * 2 + core).start()
+
+        each(q, give_back)
+        if q == 0:
+            keep_back.start()
+        share.wait_send()
+        give.wait_send()
+    keep_back.wait()
+    others = pl.ds(0, 31)
+    remote(summed.at[others], back.at[others], rs_sem, back_sem, ctx=me).wait_recv()
+    gathered = back[...].reshape(32 * CAP, -1)
+    result = (dot(hi[...], gathered) + dot(lo[...], gathered)).astype(bf16)
+    width = moe.shape[-1]
+    for k in range(4):
+        moe[k] = result[:, k * width : (k + 1) * width]
+    copies = []
+    for dy in range(1, 4):
+        to = (y + dy) % 4
+        copies.append(remote(moe.at[to], landed.at[y], ms_sem.at[dy - 1], mr_sem.at[dy - 1], ch=to))
+        copies[-1].start()
+    landed[y] = moe[y]
+    for copy in copies:
+        copy.wait()
+    out[...] = landed[...].reshape(out.shape)
+    remote(send.at[others], got.at[others], send_sem, got_sem.at[0], ctx=me).wait_send()
+    remote(summed.at[others], back.at[others], rs_sem, back_sem, ctx=me).wait_send()
 
 
 def call(kernel, out_shape, *args, scratch=()):
@@ -170,30 +292,31 @@
         routes,
         routes.T,
     )
-    same_side = [[2 * e + side for e in range(shards // 2)] for side in range(2)]
-    swap = [(i, i ^ 1) for i in range(shards)]
-
-    def exchange(block):
-        out = lax.all_to_all(
-            block.reshape(experts, CAP, width),
-            "ctx",
-            split_axis=0,
-            concat_axis=0,
-            axis_index_groups=same_side,
-            tiled=True,
-        )
-        return out.reshape(slots, width)
-
-    mine = exchange(send)
-    theirs = lax.ppermute(mine, "ctx", swap)
-    up, down = w_up[0], w_down[0]
-    out_theirs = call(expert_kernel, shape((slots, width), bf16), theirs, up, down)
-    partner_part = lax.ppermute(out_theirs, "ctx", swap)
-    out_mine = call(expert_kernel, shape((slots, width), bf16), mine, up, down)
-    summed = (out_mine.astype(f32) + partner_part.astype(f32)).astype(bf16)
-    back = exchange(summed)
-    moe_rows = call(combine_kernel, shape((rows, width), bf16), hi, lo, back)
-    moe_out = lax.all_to_all(moe_rows, "ch", split_axis=1, concat_axis=0, tiled=True)
+    blocks = (experts, CAP, width)
+    dma = pltpu.SemaphoreType.DMA
+    moe_out = pl.pallas_call(
+        experts_kernel,
+        out_shape=shape((tok_dev, ch_dev), bf16),
+        in_specs=[pl.BlockSpec(memory_space=pltpu.VMEM)] * 5,
+        out_specs=pl.BlockSpec(memory_space=pltpu.VMEM),
+        scratch_shapes=[pltpu.VMEM(blocks, bf16)] * 6
+        + [pltpu.VMEM((4, rows, ch_dev), bf16)] * 2
+        + [
+            pltpu.VMEM((rows, width), f32),
+            dma,
+            dma((4,)),
+            dma((4,)),
+            dma((4,)),
+            dma((4,)),
+            dma((4,)),
+            dma,
+            dma,
+            dma((3,)),
+            dma((3,)),
+            dma((2,)),
+        ],
+        compiler_params=pltpu.CompilerParams(collective_id=0, has_side_effects=True),
+    )(send.reshape(blocks), hi, lo, w_up[0], w_down[0])
     return (mixed, moe_out)
 
 

time: 167 us -> 135 us (0.81); the launches traced: 165 us -> 135 us
  blocking collectives: 100 us -> 30.6 us
  Pallas kernels: 18.9 us -> 66.5 us
  starting transfers between devices: 13.8 us -> 10 us
  waiting for transfers between devices: 19.2 us -> 16.1 us
    all_to_all x3 -> x0, blocking collectives: 69.6 us -> none  [the longest x2 61.7 us: exchange(): lax.all_to_all(block.reshape(experts, CAP, width), 'ctx', split_axis=0, c...]
    pallas_call x0 -> x1, Pallas kernels: none -> 57.6 us  [body(): pl.pallas_call(experts_kernel, out_shape=shape((tok_dev, ch_dev), bf16),...]
    pallas_call x5 -> x2, Pallas kernels: 18.9 us -> 8.87 us  [call(): pl.pallas_call(kernel, out_shape=out_shape, in_specs=[pl.BlockSpec(memory...]
    ppermute x2 -> x0, starting transfers between devices: 3.97 us -> none  [the longest x1 3.59 us: body(): theirs = lax.ppermute(mine, 'ctx', swap)]
    ppermute x2 -> x0, waiting for transfers between devices: 2.29 us -> none  [the longest x1 2.29 us: body(): theirs = lax.ppermute(mine, 'ctx', swap)]
    unnamed x20 -> x16, local copies, waits for them, and re-layouts: 4.59 us -> 6.23 us
  transfers between devices with their start and end apart: 4 -> 2, of which waited for: 3 -> 2; matrix products, arithmetic and copies ran while one was open for 1% -> 2% of each run, Pallas kernels for 2% -> 0%
where the time goes in v2:
time: 135 us
  Pallas kernels  66.5 us (49%)
  blocking collectives  30.6 us (23%)
  waiting for transfers between devices  16.1 us (12%)
  starting transfers between devices  10 us (7%)
  local copies, waits for them, and re-layouts  9.13 us (7%)
  other arithmetic  1.49 us (1%)
    pallas_call x1, Pallas kernels, body(): pl.pallas_call(experts_kernel, out_shape=shape((tok_dev, ch_dev), bf16),...  57.6 us
    all_to_all x1, blocking collectives, body(): lax.all_to_all(packed, 'ctx', split_axis=0, concat_axis=0, tiled=True)  30.6 us
    all_to_all x1, waiting for transfers between devices, body(): lax.all_to_all(conv.reshape(shards, chans, tok_dev), 'ctx', split_axis=0,...  12 us
    pallas_call x2, Pallas kernels, call(): pl.pallas_call(kernel, out_shape=out_shape, in_specs=[pl.BlockSpec(memory...  8.87 us
    unnamed x16, local copies, waits for them, and re-layouts  6.23 us
    all_to_all x1, starting transfers between devices, body(): lax.all_to_all(conv.reshape(shards, chans, tok_dev), 'ctx', split_axis=0,...  5.69 us
    all_to_all x1, starting transfers between devices, body(): lax.all_to_all(mixed, 'ch', split_axis=0, concat_axis=1, tiled=True)  4.32 us
    all_to_all x1, waiting for transfers between devices, body(): lax.all_to_all(mixed, 'ch', split_axis=0, concat_axis=1, tiled=True)  4.16 us
  transfers between devices with their start and end apart: 2, of which 2 were waited for; matrix products, arithmetic and copies ran while one was open for 2% of the time, Pallas kernels for 0%

profile of v2, /device:TPU:1, one launch (start us, length us, event | category | flops | bytes accessed | tf_op | source)
XLA Modules:
  0.0 134.5 jit_solution(11391349790776871560)
XLA Ops:
  0.6 1.1 convert_bitcast_fusion
  1.7 0.1 copy.33
  1.8 0.0 copy-start
  1.9 0.1 reshape.27
  1.9 0.9 copy-done
  2.8 0.1 copy.32
  2.9 0.1 reshape.26
  3.0 0.3 pad_maximum_fusion
  3.3 30.6 %all_to_all.29 = bf16[64,8,512]{2,1,0:T(8,128)(2,1)} all-to-all(bf16[64,8,512]{2,1,0:T(8,128)(2,1)S(1)} %pad_maximum_fusion), channel_id=1, replica_groups=mesh['ctx'=64,'ch'=4] {'ctx'}, dimensions={0} | all-to-all | bytes 1048576 | tf_op jit(solution)/shard_map/all_to_all | solution.py:270
  33.9 5.3 %shard_map.158 = bf16[256,512]{1,0:T(8,128)(2,1)} custom-call(bf16[512,512]{1,0:T(8,128)(2,1)} %bitcast.19, bf16[128,512]{1,0:T(8,128)(2,1)} %constant.12.clone.refs_1_, f32[64,512]{1,0:T(8,128)} %constant.13.clone.refs_2_, f32[64,512]{1,0:T(8,128)} %constant.14.clone.refs_3_, bf16[512,512]{1,0:T(8,128)(2,1)} %constant.15.clone.refs_4_, ...), custom_call_target="tpu_custom_call" | custom-call | tf_op jit(solution)/shard_map/pallas_call | solution.py:249
  39.1 1.7 %reshape.29 = bf16[64,4,512]{2,1,0:T(4,128)(2,1)} reshape(bf16[256,512]{1,0:T(8,128)(2,1)} %shard_map.158) | data formatting | bytes 524288 | tf_op jit(solution)/shard_map/reshape | solution.py:279
  40.9 5.7 %all-to-all-start.1 = ((bf16[64,4,512]{2,1,0:T(4,128)(2,1)}), bf16[64,4,512]{2,1,0:T(4,128)(2,1)S(1)}, u32[]{:S(2)}, u32[]{:S(2)}) async-start(bf16[64,4,512]{2,1,0:T(4,128)(2,1)} %reshape.29), calls=%async_computation.1 | async-start | bytes 524288 | tf_op jit(solution)/shard_map/all_to_all | solution.py:278
  46.6 0.0 copy-start.1
  46.6 0.1 copy.34
  46.7 0.8 copy-done.1
  47.5 0.1 copy.31
  47.7 0.0 copy-start.4
  47.7 12.0 %all-to-all-done.1 = bf16[64,4,512]{2,1,0:T(4,128)(2,1)S(1)} async-done(((bf16[64,4,512]{2,1,0:T(4,128)(2,1)}), bf16[64,4,512]{2,1,0:T(4,128)(2,1)S(1)}, u32[]{:S(2)}, u32[]{:S(2)}) %all-to-all-start.1) | async-done | bytes 262176 | tf_op jit(solution)/shard_map/all_to_all | solution.py:278
  59.7 0.0 copy-done.4
  59.7 0.2 fusion.1
  59.8 0.8 copy.39
  60.7 0.0 copy-start.3
  60.7 0.0 copy-start.2
  60.7 4.3 %all-to-all-start.2 = ((bf16[4,128,256]{2,1,0:T(8,128)(2,1)}), bf16[4,128,256]{2,1,0:T(8,128)(2,1)S(1)}, u32[]{:S(2)}, u32[]{:S(2)}) async-start(bf16[4,128,256]{2,1,0:T(8,128)(2,1)} %bitcast.4), calls=%async_computation.2 | async-start | bytes 524288 | tf_op jit(solution)/shard_map/all_to_all | solution.py:283
  65.0 0.0 copy-done.3
  65.0 0.7 copy.38.refs_3_
  65.7 0.0 copy-done.2
  65.7 1.0 copy.37.refs_2_
  66.8 4.2 %all-to-all-done.2 = bf16[4,128,256]{2,1,0:T(8,128)(2,1)S(1)} async-done(((bf16[4,128,256]{2,1,0:T(8,128)(2,1)}), bf16[4,128,256]{2,1,0:T(8,128)(2,1)S(1)}, u32[]{:S(2)}, u32[]{:S(2)}) %all-to-all-start.2) | async-done | bytes 262176 | tf_op jit(solution)/shard_map/all_to_all | solution.py:283
  70.9 0.7 copy.41
  71.7 3.6 %shard_map.159 = (bf16[512,1024]{1,0:T(8,128)(2,1)}, bf16[128,512]{1,0:T(8,128)(2,1)}, bf16[128,512]{1,0:T(8,128)(2,1)}) custom-call(bf16[128,1024]{1,0:T(8,128)(2,1)} %bitcast.23, f32[1,1024]{1,0:T(1,128)} %bitcast.26, f32[1024,32]{1,0:T(8,128)} %copy.37.refs_2_, s32[128,2]{1,0:T(8,128)} %copy.38.refs_3_, s32[2,128]{1,0:T(2,128)} %bitcast.27), custom_call_target="tpu_custom_call" | custom-call | tf_op jit(solution)/shard_map/pallas_call | solution.py:249
  75.3 57.6 %shard_map.160 = bf16[512,256]{1,0:T(8,128)(2,1)} custom-call(bf16[32,16,1024]{2,1,0:T(8,128)(2,1)} %bitcast.20, bf16[128,512]{1,0:T(8,128)(2,1)} %get-tuple-element.6.hi, bf16[128,512]{1,0:T(8,128)(2,1)} %get-tuple-element.7.lo, bf16[1024,256]{1,0:T(8,128)(2,1)} %bitcast.24, bf16[256,1024]{1,0:T(8,128)(2,1)} %bitcast.25), custom_call_target="tpu_custom_call" | custom-call | tf_op jit(solution)/shard_map/pallas_call | solution.py:297
  132.9 1.7 %copy.43 = bf16[512,256]{1,0:T(8,128)(2,1)} copy(bf16[512,256]{1,0:T(8,128)(2,1)} %shard_map.160) | data formatting | bytes 524288
  (1 shorter events, 0.0 us)
Async XLA Ops:
  1.8 1.0 copy-start
  40.9 18.8 %all-to-all-start.1 = ((bf16[64,4,512]{2,1,0:T(4,128)(2,1)}), bf16[64,4,512]{2,1,0:T(4,128)(2,1)S(1)}, u32[]{:S(2)}, u32[]{:S(2)}) async-start(bf16[64,4,512]{2,1,0:T(4,128)(2,1)} %reshape.29), calls=%async_computation.1 | async-start | bytes 524288 | tf_op jit(solution)/shard_map/all_to_all | solution.py:278
  46.6 1.0 copy-start.1
  47.7 12.0 %copy-start.4 = (f32[256]{0:T(256)S(1)}, f32[256]{0:T(256)}, u32[]{:S(2)}) copy-start(f32[256]{0:T(256)} %param.18) | copy-start | bytes 3076
  60.7 4.3 %copy-start.3 = (s32[128,2]{0,1:T(2,128)S(1)}, s32[128,2]{0,1:T(2,128)}, u32[]{:S(2)}) copy-start(s32[128,2]{0,1:T(2,128)} %param.23) | copy-start | bytes 3076
  60.7 5.1 %copy-start.2 = (f32[1024,32]{0,1:T(8,128)S(1)}, f32[1024,32]{0,1:T(8,128)}, u32[]{:S(2)}) copy-start(f32[1024,32]{0,1:T(8,128)} %param.20) | copy-start | bytes 393220
  60.7 10.2 %all-to-all-start.2 = ((bf16[4,128,256]{2,1,0:T(8,128)(2,1)}), bf16[4,128,256]{2,1,0:T(8,128)(2,1)S(1)}, u32[]{:S(2)}, u32[]{:S(2)}) async-start(bf16[4,128,256]{2,1,0:T(8,128)(2,1)} %bitcast.4), calls=%async_computation.2 | async-start | bytes 524288 | tf_op jit(solution)/shard_map/all_to_all | solution.py:283

commit v3 on v2

v3 whole, which is shorter than its diff:
```python
import math

import jax
import jax.numpy as jnp
import numpy as np
from jax import lax
from jax.experimental import pallas as pl
from jax.experimental.pallas import tpu as pltpu
from jax.sharding import PartitionSpec as P

CAP = 16
bf16 = jnp.bfloat16
f32 = jnp.float32


def dft_constants(shards, tok, chans):
    total = shards * tok
    fields = 2 * chans
    row = np.arange(shards)
    col = np.arange(tok)
    outer = 2.0 * np.pi * row[None, :] * (row[:, None] + 0.25) / shards
    first = np.concatenate([np.cos(outer), -np.sin(outer)], axis=0)
    first = np.repeat(first, fields, axis=1)
    last = np.concatenate([np.cos(outer.T), -np.sin(outer.T)], axis=1) / total
    last = np.repeat(last, fields, axis=0)
    turn = 2.0 * np.pi * (row[:, None] + 0.25) * col[None, :] / total
    inner = 2.0 * np.pi * ((col[:, None] * col[None, :]) % tok) / tok
    as16 = lambda a: jnp.asarray(a.astype(np.float32), bf16)
    as32 = lambda a: jnp.asarray(a.astype(np.float32))
    return (
        as16(first),
        as32(np.cos(turn)),
        as32(-np.sin(turn)),
        as16(np.cos(inner)),
        as16(np.sin(inner)),
        as16(last),
    )


def dot(a, b):
    return jnp.dot(a, b, preferred_element_type=f32)


def iota(shape, axis):
    return lax.broadcasted_iota(jnp.int32, shape, axis)


def one_hot(mask):
    return mask.astype(f32).astype(bf16)


def contract(a, b, axis_a, axis_b):
    return lax.dot_general(a, b, (((axis_a,), (axis_b,)), ((), ())), preferred_element_type=f32)


def pack(signal, taps, shards, fields):
    chans = fields // 2
    shape = (shards * fields, signal.shape[1])
    row, chan = iota(shape, 0), iota(shape, 1)
    field = row % fields
    mine = row // fields * chans + field % chans == chan
    sig = contract(one_hot(mine & (field < chans)), signal, 1, 1)
    tap = contract(one_hot(mine & (field >= chans)), taps.astype(bf16), 1, 1)
    return sig + tap


def convolve(data, tables, re_ref, im_ref, shards, chans):
    first, tr, ti, cos, sin, last = (table[...] for table in tables)
    fields = 2 * chans
    tok = data.shape[1]
    lane = iota(first.shape, 1) % fields
    for field in range(fields):
        g = dot(jnp.where(lane == field, first, jnp.zeros_like(first)), data)
        g_re, g_im = g[:shards], g[shards:]
        rows = pl.ds(field * shards, shards)
        re_ref[rows, :] = (g_re * tr - g_im * ti).astype(bf16)
        im_ref[rows, :] = (g_re * ti + g_im * tr).astype(bf16)
    re, im = re_ref[...], im_ref[...]
    x_re = dot(re, cos) + dot(im, sin)
    x_im = dot(im, cos) - dot(re, sin)
    half = chans * shards
    p_re = (x_re[:half] * x_re[half:] - x_im[:half] * x_im[half:]).astype(bf16)
    p_im = (x_re[:half] * x_im[half:] + x_im[:half] * x_re[half:]).astype(bf16)
    g_re = dot(p_re, cos) - dot(p_im, sin)
    g_im = dot(p_im, cos) + dot(p_re, sin)
    row = iota(last.shape, 0) % fields
    total = jnp.zeros((shards * fields, tok // 2), f32)
    for chan in range(chans):
        rows = slice(chan * shards, (chan + 1) * shards)
        a = (g_re[rows] * tr + g_im[rows] * ti).astype(bf16)
        b = (g_im[rows] * tr - g_re[rows] * ti).astype(bf16)
        both = jnp.concatenate([a, b], axis=0)
        for side in range(2):
            table = jnp.where(row == side * chans + chan, last, jnp.zeros_like(last))
            total += dot(table, both[:, side * (tok // 2) : (side + 1) * (tok // 2)])
    return total


def unpack(data, side, fields):
    chans = fields // 2
    shape = (data.shape[0], data.shape[0] // fields * chans)
    row, chan = iota(shape, 0), iota(shape, 1)
    field = row % fields
    mine = (row // fields * chans + field % chans == chan) & (field // chans == side)
    return contract(data, one_hot(mine), 0, 0)


def route(x, gain, router, routes, routes_t):
    count = x.shape[0]
    experts = router.shape[1]
    slots = experts * CAP
    scale = lax.rsqrt(jnp.mean(x * x, axis=-1, keepdims=True) + 1e-05)
    normed = (x * scale * gain).astype(bf16)
    logits = jnp.dot(
        normed.astype(f32), router, precision=lax.Precision.HIGHEST, preferred_element_type=f32
    )
    gates = jax.nn.sigmoid(logits)
    g_hi = gates.astype(bf16)
    g_lo = (gates - g_hi.astype(f32)).astype(bf16)
    ids = iota((count, experts), 1)
    named = one_hot((routes[:, 0:1] == ids) | (routes[:, 1:2] == ids))
    rows, cols = iota((count, count), 0), iota((count, count), 1)
    rank = dot(one_hot(cols < rows), named).astype(bf16)
    spread = one_hot(iota((experts, slots), 1) // CAP == iota((experts, slots), 0))
    slot = (iota((count, slots), 1) % CAP).astype(f32)
    here = (dot(named, spread) > 0.5) & (dot(rank, spread) == slot)
    hi = jnp.where(here, dot(g_hi, spread), 0.0).astype(bf16)
    lo = jnp.where(here, dot(g_lo, spread), 0.0).astype(bf16)
    ids_t = iota((experts, count), 0)
    named_t = one_hot((routes_t[0:1, :] == ids_t) | (routes_t[1:2, :] == ids_t))
    rank_t = dot(named_t, one_hot(rows < cols)).astype(bf16)
    spread_t = one_hot(iota((slots, experts), 0) // CAP == iota((slots, experts), 1))
    slot_t = (iota((slots, count), 0) % CAP).astype(f32)
    here_t = (dot(spread_t, named_t) > 0.5) & (dot(spread_t, rank_t) == slot_t)
    return dot(one_hot(here_t), normed).astype(bf16), hi, lo


def remote(src, dst, send_sem, recv_sem, **where):
    return pltpu.make_async_remote_copy(
        src_ref=src,
        dst_ref=dst,
        send_sem=send_sem,
        recv_sem=recv_sem,
        device_id=where,
        device_id_type=pl.DeviceIdType.MESH,
    )


class Place:
    def __init__(self, zs=8, xs=4):
        self.zs, self.xs = zs, xs
        self.me = lax.axis_index("ctx")
        self.y = lax.axis_index("ch")
        self.core = self.me % 2
        self.chip = self.me // 2
        self.z = self.chip // xs
        self.x = self.chip % xs
        self.twin = self.me + 1 - 2 * self.core

    def at(self, dz, dx):
        return (self.z + dz + self.zs) % self.zs * self.xs + (self.x + dx + self.xs) % self.xs


def greet(place, count, ys):
    barrier = pltpu.get_barrier_semaphore()

    def tell(**where):
        pl.semaphore_signal(barrier, inc=1, device_id=where, device_id_type=pl.DeviceIdType.MESH)

    def shard(i, carry):
        tell(ctx=(place.me + i) % count)
        return carry

    lax.fori_loop(1, count, shard, 0)
    for dy in range(1, ys):
        tell(ch=(place.y + dy) % ys)
    return lambda: pl.semaphore_wait(barrier, count - 1 + ys - 1)


def offsets(q, half, j):
    if half == 0:
        return 4 - q, j
    return (4 + q if q else 0), (j + 1) % 4


def each(q, act):
    for half in range(2):

        def one(j, carry):
            dz, dx = offsets(q, half, j)
            act(q * 8 + half * 4 + j, dz, dx)
            return carry

        lax.fori_loop(0, 3 if q == 0 and half == 1 else 4, one, 0)


def split(refs, far, outs, conv, moe, sems):
    refs = list(refs)
    cut = [refs[:far], refs[far : far + outs]]
    rest = refs[far + outs :]
    first = rest[:conv]
    cut.append((first[: far + 1], *first[far + 1 :]))
    cut.append(rest[conv : conv + moe])
    cut.append(rest[conv + moe :])
    return cut


def layer_kernel(
    signal, taps, skip, gain, router, routes, routes_t, gate_hbm, *rest
):
    place = Place()
    me, core, chip, y = place.me, place.core, place.chip, place.y
    (
        far, (mixed_out, out),
        (near, packed, fields, re_ref, im_ref, conv_out, conv_in, mixed, full),
        (send, hi, lo, got, twin_got, part, twin_part, summed, back, moe, landed, own),
        (far_sem, local_sem, conv_sem, xs_sem, xr_sem, send_sem, got_sem, fs_sem, fr_sem, ps_sem, pr_sem,
         rs_sem, back_sem, ms_sem, mr_sem),
    ) = split(rest, 8, 2, 17, 12, 15)
    shards, width_ch = 64, signal.shape[1]
    chans = width_ch // shards
    ready = greet(place, shards, 4)
    fetches = [
        pltpu.make_async_copy(a, b, far_sem.at[i]) for i, (a, b) in enumerate(zip((gate_hbm, *far), near))
    ]
    for fetch in fetches:
        fetch.start()
    gate, tables, up_ref, down_ref = near[0], near[1:7], near[7], near[8]
    packed[...] = pack(signal[...], taps[...], shards, 2 * chans).reshape(packed.shape).astype(bf16)
    ready()

    def spread_out(source, target, ss, rs):
        def both(to):
            for side in range(2):
                where = to * 2 + side
                remote(source.at[where], target.at[me], ss, rs, ctx=where).start()

        for q in range(4):
            each(q, lambda slot, dz, dx: both(place.at(dz, dx)))
        remote(source.at[place.twin], target.at[me], ss, rs, ctx=place.twin).start()
        stay = pltpu.make_async_copy(source.at[me], target.at[me], local_sem.at[2])
        stay.start()
        most = pl.ds(0, shards - 1)
        whole = remote(source.at[most], target.at[most], ss, rs, ctx=place.twin)
        whole.wait_recv()
        stay.wait()
        return whole

    whole = spread_out(packed, fields, conv_sem.at[0], conv_sem.at[1])
    for fetch in fetches:
        fetch.wait()
    data = fields[...].astype(f32).reshape(shards * 2 * chans, -1).astype(bf16)
    total = convolve(data, tables, re_ref, im_ref, shards, chans)
    conv_out[...] = total.reshape(conv_out.shape).astype(bf16)
    whole_back = spread_out(conv_out, conv_in, conv_sem.at[2], conv_sem.at[3])
    whole.wait_send()
    data = conv_in[...].astype(f32).reshape(shards * 2 * chans, -1).astype(bf16)
    for side in range(2):
        conv = unpack(data, side, 2 * chans)
        count = conv.shape[0]
        span = slice(side * count, (side + 1) * count)
        sig = signal[span, :].astype(f32)
        value = (gate[span, :].astype(f32) * (conv + skip[...] * sig)).astype(bf16)
        mixed_out[span, :] = value
        mixed[2 * side] = value[: count // 2]
        mixed[2 * side + 1] = value[count // 2 :]
    copies = []
    for dy in range(1, 4):
        to = (y + dy) % 4
        copies.append(remote(mixed.at[to], full.at[y], xs_sem.at[dy - 1], xr_sem.at[dy - 1], ch=to))
        copies[-1].start()
    full[y] = mixed[y]
    for copy in copies:
        copy.wait()
    whole_back.wait_send()
    x = jnp.concatenate([full[k] for k in range(4)], axis=1).astype(f32)
    rows_out, hi[...], lo[...] = route(x, gain[...], router[...], routes[...], routes_t[...])
    send[...] = rows_out.reshape(send.shape)
    chunk = 8
    rows = chunk * CAP
    for q in range(4):

        def dispatch(slot, dz, dx):
            to = place.at(dz, dx)
            remote(send.at[to], got.at[slot], send_sem, got_sem.at[q], ctx=to * 2 + core).start()

        each(q, dispatch)
    keep = pltpu.make_async_copy(send.at[chip], got.at[7], local_sem.at[0])
    keep.start()
    keep_back = pltpu.make_async_copy(summed.at[7], back.at[chip], local_sem.at[1])

    def mlp(block):
        x = block.reshape(rows, block.shape[-1])
        hidden = jax.nn.gelu(dot(x, up_ref[...]), approximate=True).astype(bf16)
        return dot(hidden, down_ref[...])

    for q in range(4):
        slots = pl.ds(q * chunk, chunk)
        here = pl.ds(q * chunk, 7) if q == 0 else slots
        remote(send.at[here], got.at[here], send_sem, got_sem.at[q], ctx=me).wait_recv()
        if q == 0:
            keep.wait()
        share = remote(got.at[slots], twin_got.at[slots], fs_sem.at[q], fr_sem.at[q], ctx=place.twin)
        share.start()
        own[...] = mlp(got[slots])
        share.wait_recv()
        part[slots] = mlp(twin_got[slots]).astype(bf16).reshape(chunk, CAP, -1)
        give = remote(part.at[slots], twin_part.at[slots], ps_sem.at[q], pr_sem.at[q], ctx=place.twin)
        give.start()
        give.wait_recv()
        total = own[...].reshape(chunk, CAP, -1) + twin_part[slots].astype(f32)
        summed[slots] = total.astype(bf16)

        def give_back(slot, dz, dx):
            to = place.at(-dz, -dx)
            remote(summed.at[slot], back.at[chip], rs_sem, back_sem, ctx=to * 2 + core).start()

        each(q, give_back)
        if q == 0:
            keep_back.start()
        share.wait_send()
        give.wait_send()
    keep_back.wait()
    others = pl.ds(0, 31)
    remote(summed.at[others], back.at[others], rs_sem, back_sem, ctx=me).wait_recv()
    gathered = back[...].reshape(32 * CAP, -1)
    result = (dot(hi[...], gathered) + dot(lo[...], gathered)).astype(bf16)
    width = moe.shape[-1]
    for k in range(4):
        moe[k] = result[:, k * width : (k + 1) * width]
    copies = []
    for dy in range(1, 4):
        to = (y + dy) % 4
        copies.append(remote(moe.at[to], landed.at[y], ms_sem.at[dy - 1], mr_sem.at[dy - 1], ch=to))
        copies[-1].start()
    landed[y] = moe[y]
    for copy in copies:
        copy.wait()
    out[...] = landed[...].reshape(out.shape)
    remote(send.at[others], got.at[others], send_sem, got_sem.at[0], ctx=me).wait_send()
    remote(summed.at[others], back.at[others], rs_sem, back_sem, ctx=me).wait_send()


def call(kernel, out_shape, *args, scratch=()):
    return pl.pallas_call(
        kernel,
        out_shape=out_shape,
        in_specs=[pl.BlockSpec(memory_space=pltpu.VMEM)] * len(args),
        out_specs=jax.tree.map(lambda _: pl.BlockSpec(memory_space=pltpu.VMEM), out_shape),
        scratch_shapes=list(scratch),
    )(*args)


def body(signal, gate_v, taps, skip, norm_gain, router, w_up, w_down, routes):
    tok_dev, ch_dev = signal.shape
    shards = lax.axis_size("ctx")
    groups = lax.axis_size("ch")
    chans = ch_dev // shards
    experts = router.shape[1]
    width = norm_gain.shape[0]
    rows = tok_dev // groups
    shape = jax.ShapeDtypeStruct
    far = (*dft_constants(shards, tok_dev, chans), w_up[0], w_down[0])
    blocks = (experts, CAP, width)
    dma = pltpu.SemaphoreType.DMA
    vmem = pltpu.VMEM
    here = pl.BlockSpec(memory_space=vmem)
    there = pl.BlockSpec(memory_space=pl.ANY)
    local = shape((tok_dev, ch_dev), bf16)
    mixed, moe_out = pl.pallas_call(
        layer_kernel,
        out_shape=(local, local),
        in_specs=[here] * 7 + [there] * (1 + len(far)),
        out_specs=(here, here),
        scratch_shapes=[vmem(gate_v.shape, gate_v.dtype)]
        + [vmem(a.shape, a.dtype) for a in far]
        + [vmem((shards, 2 * chans, tok_dev), bf16)] * 2
        + [vmem((2 * chans * shards, tok_dev), bf16)] * 2
        + [vmem((shards, 2 * chans, tok_dev // 2), bf16)] * 2
        + [vmem((groups, rows, ch_dev), bf16)] * 2
        + [vmem(blocks, bf16)]
        + [vmem((rows, experts * CAP), bf16)] * 2
        + [vmem(blocks, bf16)] * 6
        + [vmem((groups, rows, ch_dev), bf16)] * 2
        + [vmem((rows, width), f32)]
        + [dma((9,)), dma((3,)), dma((4,)), dma((3,)), dma((3,)), dma]
        + [dma((4,))] * 5
        + [dma, dma, dma((3,)), dma((3,))],
        compiler_params=pltpu.CompilerParams(collective_id=0, has_side_effects=True),
    )(signal, taps, skip[None, :], norm_gain[None, :], router, routes, routes.T, gate_v, *far)
    return (mixed, moe_out)


def solution(mesh):
    in_specs = (
        P("ctx", "ch"),
        P("ctx", "ch"),
        P("ctx", "ch"),
        P("ch"),
        P(),
        P(),
        P("ctx", None, None),
        P("ctx", None, None),
        P(("ctx", "ch"), None),
    )
    out_specs = (P("ctx", "ch"), P("ctx", "ch"))
    return jax.shard_map(body, mesh=mesh, in_specs=in_specs, out_specs=out_specs, check_vma=False)
```

time: 135 us -> 108 us (0.80)
  Pallas kernels: 66.5 us -> 102 us
  blocking collectives: 30.6 us -> 0 us
  waiting for transfers between devices: 16.1 us -> 0 us
  starting transfers between devices: 10 us -> 0 us
  local copies, waits for them, and re-layouts: 9.13 us -> 5.73 us
  other arithmetic: 1.49 us -> 0 us
    pallas_call x3 -> x1, Pallas kernels: 66.5 us -> 102 us  [body(): pl.pallas_call(layer_kernel, out_shape=(local, local), in_specs=[here] *...]
    all_to_all x1 -> x0, blocking collectives: 30.6 us -> none  [body(): lax.all_to_all(packed, 'ctx', split_axis=0, concat_axis=0, tiled=True)]
    all_to_all x2 -> x0, waiting for transfers between devices: 16.1 us -> none  [the longest x1 12 us: body(): lax.all_to_all(conv.reshape(shards, chans, tok_dev), 'ctx', split_axis=0,...]
    all_to_all x2 -> x0, starting transfers between devices: 10 us -> none  [the longest x1 5.69 us: body(): lax.all_to_all(conv.reshape(shards, chans, tok_dev), 'ctx', split_axis=0,...]
    reshape x3 -> x0, local copies, waits for them, and re-layouts: 1.85 us -> none  [the longest x1 1.72 us: body(): conv.reshape(shards, chans, tok_dev)]
    unnamed x16 -> x8, local copies, waits for them, and re-layouts: 6.23 us -> 5.73 us
  transfers between devices with their start and end apart: 2 -> 0, of which waited for: 2 -> 0; matrix products, arithmetic and copies ran while one was open for 2% -> 0% of each run, Pallas kernels for 0% -> 0%
where the time goes in v3:
time: 108 us
  Pallas kernels  102 us (94%)
  local copies, waits for them, and re-layouts  5.73 us (5%)
    pallas_call x1, Pallas kernels, body(): pl.pallas_call(layer_kernel, out_shape=(local, local), in_specs=[here] *...  102 us
    unnamed x8, local copies, waits for them, and re-layouts  5.73 us

profile of v3, /device:TPU:1, one launch (start us, length us, event | category | flops | bytes accessed | tf_op | source)
XLA Modules:
  0.0 108.3 jit_solution(12963658066293760284)
XLA Ops:
  0.6 0.0 copy-start.1
  0.6 0.7 copy-done.1
  1.3 0.7 copy.18.routes
  2.1 1.9 %copy.17.router = f32[1024,32]{1,0:T(8,128)} copy(f32[1024,32]{0,1:T(8,128)} %param.20) | data formatting | bytes 262144 | tf_op args[5]
  4.0 101.9 %shard_map.158 = (bf16[512,256]{1,0:T(8,128)(2,1)}, bf16[512,256]{1,0:T(8,128)(2,1)}) custom-call(bf16[512,256]{1,0:T(8,128)(2,1)} %signal.1, f32[512,256]{1,0:T(8,128)} %taps.1, f32[1,256]{1,0:T(1,128)} %bitcast.9, f32[1,1024]{1,0:T(1,128)} %bitcast.7, f32[1024,32]{1,0:T(8,128)} %copy.17.router, s32[128,2]{1,0:T(8,128)} %copy.18.routes, s32[2,128]{1,0:T(2,128)} %bitcast.8, ...), custom_call_target="tpu_custom_call" | custom-call | tf_op jit(solution)/shard_map/pallas_call | solution.py:370
  105.9 0.0 copy-start
  105.9 1.7 %copy.21 = bf16[512,256]{1,0:T(8,128)(2,1)} copy(bf16[512,256]{1,0:T(8,128)(2,1)} %get-tuple-element.4) | data formatting | bytes 524288
  107.6 0.0 copy-done
  107.6 0.7 copy.22
Async XLA Ops:
  0.6 0.7 copy-start.1
  105.9 1.7 %copy-start = (bf16[512,256]{1,0:T(8,128)(2,1)S(1)}, bf16[512,256]{1,0:T(8,128)(2,1)}, u32[]{:S(2)}) copy-start(bf16[512,256]{1,0:T(8,128)(2,1)} %get-tuple-element.5) | copy-start | bytes 786436

commit v4 on v3

--- a/solution.py
+++ b/solution.py
@@ -105,34 +105,41 @@
     return contract(data, one_hot(mine), 0, 0)
 
 
-def route(x, gain, router, routes, routes_t):
-    count = x.shape[0]
-    experts = router.shape[1]
+def slots_of(routes_t, experts):
+    count = routes_t.shape[1]
     slots = experts * CAP
+    ids = iota((experts, count), 0)
+    named = one_hot((routes_t[0:1, :] == ids) | (routes_t[1:2, :] == ids))
+    rank = dot(named, one_hot(iota((count, count), 0) < iota((count, count), 1))).astype(bf16)
+    spread = one_hot(iota((slots, experts), 0) // CAP == iota((slots, experts), 1))
+    slot = (iota((slots, count), 0) % CAP).astype(f32)
+    return one_hot((dot(spread, named) > 0.5) & (dot(spread, rank) == slot))
+
+
+def normalize(x, gain):
     scale = lax.rsqrt(jnp.mean(x * x, axis=-1, keepdims=True) + 1e-05)
-    normed = (x * scale * gain).astype(bf16)
-    logits = jnp.dot(
-        normed.astype(f32), router, precision=lax.Precision.HIGHEST, preferred_element_type=f32
+    return (x * scale * gain).astype(bf16)
+
+
+def gates_of(normed, router_t, here):
+    count = normed.shape[0]
+    experts = router_t.shape[0]
+    slots = experts * CAP
+    logits = lax.dot_general(
+        router_t,
+        normed.astype(f32),
+        (((1,), (1,)), ((), ())),
+        precision=lax.Precision.HIGHEST,
+        preferred_element_type=f32,
     )
     gates = jax.nn.sigmoid(logits)
-    g_hi = gates.astype(bf16)
-    g_lo = (gates - g_hi.astype(f32)).astype(bf16)
-    ids = iota((count, experts), 1)
-    named = one_hot((routes[:, 0:1] == ids) | (routes[:, 1:2] == ids))
-    rows, cols = iota((count, count), 0), iota((count, count), 1)
-    rank = dot(one_hot(cols < rows), named).astype(bf16)
-    spread = one_hot(iota((experts, slots), 1) // CAP == iota((experts, slots), 0))
-    slot = (iota((count, slots), 1) % CAP).astype(f32)
-    here = (dot(named, spread) > 0.5) & (dot(rank, spread) == slot)
-    hi = jnp.where(here, dot(g_hi, spread), 0.0).astype(bf16)
-    lo = jnp.where(here, dot(g_lo, spread), 0.0).astype(bf16)
-    ids_t = iota((experts, count), 0)
-    named_t = one_hot((routes_t[0:1, :] == ids_t) | (routes_t[1:2, :] == ids_t))
-    rank_t = dot(named_t, one_hot(rows < cols)).astype(bf16)
-    spread_t = one_hot(iota((slots, experts), 0) // CAP == iota((slots, experts), 1))
-    slot_t = (iota((slots, count), 0) % CAP).astype(f32)
-    here_t = (dot(spread_t, named_t) > 0.5) & (dot(spread_t, rank_t) == slot_t)
-    return dot(one_hot(here_t), normed).astype(bf16), hi, lo
+    high = gates.astype(bf16)
+    low = (gates - high.astype(f32)).astype(bf16)
+    spread = one_hot(iota((slots, experts), 0) // CAP == iota((slots, experts), 1))
+    turn = one_hot(iota((count, count), 0) == iota((count, count), 1))
+    chosen = here > 0.5
+    parts = (jnp.where(chosen, dot(spread, part), 0.0).astype(bf16) for part in (high, low))
+    return tuple(contract(turn, part, 1, 1).astype(bf16) for part in parts)
 
 
 def remote(src, dst, send_sem, recv_sem, **where):
@@ -206,17 +213,17 @@
 
 
 def layer_kernel(
-    signal, taps, skip, gain, router, routes, routes_t, gate_hbm, *rest
+    signal, taps, skip, gain, router_t, routes_t, gate_hbm, *rest
 ):
     place = Place()
     me, core, chip, y = place.me, place.core, place.chip, place.y
     (
         far, (mixed_out, out),
         (near, packed, fields, re_ref, im_ref, conv_out, conv_in, mixed, full),
-        (send, hi, lo, got, twin_got, part, twin_part, summed, back, moe, landed, own),
+        (send, here, got, twin_got, part, twin_part, summed, back, moe, landed, own),
         (far_sem, local_sem, conv_sem, xs_sem, xr_sem, send_sem, got_sem, fs_sem, fr_sem, ps_sem, pr_sem,
          rs_sem, back_sem, ms_sem, mr_sem),
-    ) = split(rest, 8, 2, 17, 12, 15)
+    ) = split(rest, 8, 2, 17, 11, 15)
     shards, width_ch = 64, signal.shape[1]
     chans = width_ch // shards
     ready = greet(place, shards, 4)
@@ -227,6 +234,7 @@
         fetch.start()
     gate, tables, up_ref, down_ref = near[0], near[1:7], near[7], near[8]
     packed[...] = pack(signal[...], taps[...], shards, 2 * chans).reshape(packed.shape).astype(bf16)
+    here[...] = slots_of(routes_t[...], router_t.shape[0])
     ready()
 
     def spread_out(source, target, ss, rs):
@@ -262,20 +270,19 @@
         sig = signal[span, :].astype(f32)
         value = (gate[span, :].astype(f32) * (conv + skip[...] * sig)).astype(bf16)
         mixed_out[span, :] = value
-        mixed[2 * side] = value[: count // 2]
-        mixed[2 * side + 1] = value[count // 2 :]
-    copies = []
-    for dy in range(1, 4):
-        to = (y + dy) % 4
-        copies.append(remote(mixed.at[to], full.at[y], xs_sem.at[dy - 1], xr_sem.at[dy - 1], ch=to))
-        copies[-1].start()
+        for k in range(2 * side, 2 * side + 2):
+            mixed[k] = value[(k % 2) * (count // 2) : (k % 2 + 1) * (count // 2)]
+
+            @pl.when(y != k)
+            def _():
+                remote(mixed.at[k], full.at[y], xs_sem, xr_sem, ch=k).start()
+
     full[y] = mixed[y]
-    for copy in copies:
-        copy.wait()
-    whole_back.wait_send()
-    x = jnp.concatenate([full[k] for k in range(4)], axis=1).astype(f32)
-    rows_out, hi[...], lo[...] = route(x, gain[...], router[...], routes[...], routes_t[...])
-    send[...] = rows_out.reshape(send.shape)
+    trio = pl.ds(0, 3)
+    quarters = remote(mixed.at[trio], full.at[trio], xs_sem, xr_sem, ch=(y + 1) % 4)
+    quarters.wait_recv()
+    normed = normalize(jnp.concatenate([full[k] for k in range(4)], axis=1).astype(f32), gain[...])
+    send[...] = dot(here[...], normed).astype(bf16).reshape(send.shape)
     chunk = 8
     rows = chunk * CAP
     for q in range(4):
@@ -288,6 +295,9 @@
     keep = pltpu.make_async_copy(send.at[chip], got.at[7], local_sem.at[0])
     keep.start()
     keep_back = pltpu.make_async_copy(summed.at[7], back.at[chip], local_sem.at[1])
+    hi, lo = gates_of(normed, router_t[...], here[...])
+    quarters.wait_send()
+    whole_back.wait_send()
 
     def mlp(block):
         x = block.reshape(rows, block.shape[-1])
@@ -296,8 +306,8 @@
 
     for q in range(4):
         slots = pl.ds(q * chunk, chunk)
-        here = pl.ds(q * chunk, 7) if q == 0 else slots
-        remote(send.at[here], got.at[here], send_sem, got_sem.at[q], ctx=me).wait_recv()
+        came = pl.ds(q * chunk, 7) if q == 0 else slots
+        remote(send.at[came], got.at[came], send_sem, got_sem.at[q], ctx=me).wait_recv()
         if q == 0:
             keep.wait()
         share = remote(got.at[slots], twin_got.at[slots], fs_sem.at[q], fr_sem.at[q], ctx=place.twin)
@@ -324,7 +334,7 @@
     others = pl.ds(0, 31)
     remote(summed.at[others], back.at[others], rs_sem, back_sem, ctx=me).wait_recv()
     gathered = back[...].reshape(32 * CAP, -1)
-    result = (dot(hi[...], gathered) + dot(lo[...], gathered)).astype(bf16)
+    result = (dot(hi, gathered) + dot(lo, gathered)).astype(bf16)
     width = moe.shape[-1]
     for k in range(4):
         moe[k] = result[:, k * width : (k + 1) * width]
@@ -370,7 +380,7 @@
     mixed, moe_out = pl.pallas_call(
         layer_kernel,
         out_shape=(local, local),
-        in_specs=[here] * 7 + [there] * (1 + len(far)),
+        in_specs=[here] * 6 + [there] * (1 + len(far)),
         out_specs=(here, here),
         scratch_shapes=[vmem(gate_v.shape, gate_v.dtype)]
         + [vmem(a.shape, a.dtype) for a in far]
@@ -379,15 +389,15 @@
         + [vmem((shards, 2 * chans, tok_dev // 2), bf16)] * 2
         + [vmem((groups, rows, ch_dev), bf16)] * 2
         + [vmem(blocks, bf16)]
-        + [vmem((rows, experts * CAP), bf16)] * 2
+        + [vmem((experts * CAP, rows), bf16)]
         + [vmem(blocks, bf16)] * 6
         + [vmem((groups, rows, ch_dev), bf16)] * 2
         + [vmem((rows, width), f32)]
-        + [dma((9,)), dma((3,)), dma((4,)), dma((3,)), dma((3,)), dma]
+        + [dma((9,)), dma((3,)), dma((4,)), dma, dma, dma]
         + [dma((4,))] * 5
         + [dma, dma, dma((3,)), dma((3,))],
         compiler_params=pltpu.CompilerParams(collective_id=0, has_side_effects=True),
-    )(signal, taps, skip[None, :], norm_gain[None, :], router, routes, routes.T, gate_v, *far)
+    )(signal, taps, skip[None, :], norm_gain[None, :], router.T, routes.T, gate_v, *far)
     return (mixed, moe_out)
 
 

time: 108 us -> 104 us (0.963)
  local copies, waits for them, and re-layouts: 5.73 us -> 2.42 us
    unnamed x8 -> x4, local copies, waits for them, and re-layouts: 5.73 us -> 2.42 us
    pallas_call x1, Pallas kernels: 102 us -> 101 us  [body(): pl.pallas_call(layer_kernel, out_shape=(local, local), in_specs=[here] *...]
where the time goes in v4:
time: 104 us
  Pallas kernels  101 us (97%)
  local copies, waits for them, and re-layouts  2.42 us (2%)
    pallas_call x1, Pallas kernels, body(): pl.pallas_call(layer_kernel, out_shape=(local, local), in_specs=[here] *...  101 us
    unnamed x4, local copies, waits for them, and re-layouts  2.42 us

profile of v4, /device:TPU:1, one launch (start us, length us, event | category | flops | bytes accessed | tf_op | source)
XLA Modules:
  0.0 103.8 jit_solution(1601895778999475587)
XLA Ops:
  0.6 100.7 %shard_map.158 = (bf16[512,256]{1,0:T(8,128)(2,1)}, bf16[512,256]{1,0:T(8,128)(2,1)}) custom-call(bf16[512,256]{1,0:T(8,128)(2,1)} %signal.1, f32[512,256]{1,0:T(8,128)} %taps.1, f32[1,256]{1,0:T(1,128)} %bitcast.10, f32[1,1024]{1,0:T(1,128)} %bitcast.9, f32[32,1024]{1,0:T(8,128)} %bitcast.8, s32[2,128]{1,0:T(2,128)} %bitcast.11, bf16[512,256]{1,0:T(8,128)(2,1)} %gate_hbm.1, ...), custom_call_target="tpu_custom_call" | custom-call | tf_op jit(solution)/shard_map/pallas_call | solution.py:380
  101.4 0.0 copy-start
  101.4 1.7 %copy.19 = bf16[512,256]{1,0:T(8,128)(2,1)} copy(bf16[512,256]{1,0:T(8,128)(2,1)} %get-tuple-element.4) | data formatting | bytes 524288
  103.1 0.0 copy-done
  103.1 0.7 copy.20
Async XLA Ops:
  101.4 1.7 %copy-start = (bf16[512,256]{1,0:T(8,128)(2,1)S(1)}, bf16[512,256]{1,0:T(8,128)(2,1)}, u32[]{:S(2)}) copy-start(bf16[512,256]{1,0:T(8,128)(2,1)} %get-tuple-element.5) | copy-start | bytes 786436

commit v5 on v4

--- a/solution.py
+++ b/solution.py
@@ -180,8 +180,40 @@
 
     lax.fori_loop(1, count, shard, 0)
     for dy in range(1, ys):
-        tell(ch=(place.y + dy) % ys)
-    return lambda: pl.semaphore_wait(barrier, count - 1 + ys - 1)
+        other = (place.y + dy) % ys
+        tell(ch=other)
+        for dz in REACH:
+
+            def chip(i, carry):
+                tell(ctx=place.at(dz, i) * 2 + place.core, ch=other)
+                return carry
+
+            lax.fori_loop(0 if dz else 1, place.xs, chip, 0)
+    extra = (ys - 1) * (len(REACH) * place.xs - 1)
+    return lambda: pl.semaphore_wait(barrier, count - 1 + ys - 1 + extra)
+
+
+REACH = (0, 1, -1, 4)
+ORDER = (4, 0, 2, 6, 1, 7, 3, 5)
+
+
+def shift_of(y):
+    return jnp.where(y == 1, 2, jnp.where(y == 3, -2, 0))
+
+
+def nearest(d, y):
+    if d in (2, 3):
+        return 3, d - 2, (y + 1) % 4 + 4 * (d == 3)
+    if d in (5, 6):
+        return 1, d - 6, (y + 3) % 4 + 4 * (d == 5)
+    return jnp.where((y == 0) | (y == 3), 0, 2), {0: 0, 4: 4, 1: 1, 7: -1}[d], 2 * (0, 4, 1, 7).index(d) + y % 2
+
+
+def came_from(q, odd_group, y):
+    turned = y % 2 == 1
+    group = 2 * q + odd_group
+    moved = jnp.where(turned, (y - 2) * (q >= 2), (0, 4, 1, -1)[q])
+    return moved, jnp.where(turned, (group % 4 + y) % 4, (y + 3 * odd_group) % 4)
 
 
 def offsets(q, half, j):
@@ -220,10 +252,10 @@
     (
         far, (mixed_out, out),
         (near, packed, fields, re_ref, im_ref, conv_out, conv_in, mixed, full),
-        (send, here, got, twin_got, part, twin_part, summed, back, moe, landed, own),
+        (send, here, got, twin_got, part, twin_part, summed, back, moe, landed, own, stage_up, stage_down, up_ref, down_ref),
         (far_sem, local_sem, conv_sem, xs_sem, xr_sem, send_sem, got_sem, fs_sem, fr_sem, ps_sem, pr_sem,
-         rs_sem, back_sem, ms_sem, mr_sem),
-    ) = split(rest, 8, 2, 17, 11, 15)
+         rs_sem, back_sem, ms_sem, mr_sem, zs_sem, zr_sem, ys_sem, yr_sem, keep_sem),
+    ) = split(rest, 8, 2, 17, 15, 20)
     shards, width_ch = 64, signal.shape[1]
     chans = width_ch // shards
     ready = greet(place, shards, 4)
@@ -232,7 +264,45 @@
     ]
     for fetch in fetches:
         fetch.start()
-    gate, tables, up_ref, down_ref = near[0], near[1:7], near[7], near[8]
+    gate, tables, own_up, own_down = near[0], near[1:7], near[7], near[8]
+    wide, deep = own_up.shape[0] // 4, own_down.shape[0] // 4
+
+    def quarter(k):
+        return pl.ds(pl.multiple_of(k * wide, wide), wide), pl.ds(pl.multiple_of(k * deep, deep), deep)
+
+    def step_along_z(side):
+        up_rows, down_rows = quarter(y)
+        to = place.at(2 - 4 * side, 0) * 2 + core
+        return (
+            remote(own_up.at[up_rows], stage_up.at[side], zs_sem.at[side, 0], zr_sem.at[side, 0], ctx=to),
+            remote(own_down.at[down_rows], stage_down.at[side], zs_sem.at[side, 1], zr_sem.at[side, 1], ctx=to),
+        )
+
+    def step_along_y(side):
+        up_rows, down_rows = quarter(y)
+        to = 1 + 2 * side
+        return (
+            remote(stage_up.at[side], up_ref.at[up_rows], ys_sem.at[side, 0], yr_sem.at[0], ch=to),
+            remote(stage_down.at[side], down_ref.at[down_rows], ys_sem.at[side, 1], yr_sem.at[1], ch=to),
+        )
+
+    def stays(side):
+        up_rows, down_rows = quarter(y)
+        return (
+            pltpu.make_async_copy(stage_up.at[side], up_ref.at[up_rows], keep_sem.at[0]),
+            pltpu.make_async_copy(stage_down.at[side], down_ref.at[down_rows], keep_sem.at[1]),
+        )
+
+    def whole_weights():
+        return (
+            pltpu.make_async_copy(own_up, up_ref, keep_sem.at[0]),
+            pltpu.make_async_copy(own_down, down_ref, keep_sem.at[1]),
+        )
+
+    def act(copies, what):
+        for copy in copies:
+            getattr(copy, what)()
+
     packed[...] = pack(signal[...], taps[...], shards, 2 * chans).reshape(packed.shape).astype(bf16)
     here[...] = slots_of(routes_t[...], router_t.shape[0])
     ready()
@@ -257,6 +327,7 @@
     whole = spread_out(packed, fields, conv_sem.at[0], conv_sem.at[1])
     for fetch in fetches:
         fetch.wait()
+    act((*step_along_z(0), *step_along_z(1)), "start")
     data = fields[...].astype(f32).reshape(shards * 2 * chans, -1).astype(bf16)
     total = convolve(data, tables, re_ref, im_ref, shards, chans)
     conv_out[...] = total.reshape(conv_out.shape).astype(bf16)
@@ -278,6 +349,11 @@
                 remote(mixed.at[k], full.at[y], xs_sem, xr_sem, ch=k).start()
 
     full[y] = mixed[y]
+    act((*step_along_z(0), *step_along_z(1)), "wait")
+    for side in range(2):
+        pl.when(y != 1 + 2 * side)(lambda: act(step_along_y(side), "start"))
+        pl.when(y == 1 + 2 * side)(lambda: act(stays(side), "start"))
+    pl.when(y % 2 == 0)(lambda: act(whole_weights(), "start"))
     trio = pl.ds(0, 3)
     quarters = remote(mixed.at[trio], full.at[trio], xs_sem, xr_sem, ch=(y + 1) % 4)
     quarters.wait_recv()
@@ -285,19 +361,41 @@
     send[...] = dot(here[...], normed).astype(bf16).reshape(send.shape)
     chunk = 8
     rows = chunk * CAP
-    for q in range(4):
-
-        def dispatch(slot, dz, dx):
-            to = place.at(dz, dx)
-            remote(send.at[to], got.at[slot], send_sem, got_sem.at[q], ctx=to * 2 + core).start()
-
-        each(q, dispatch)
-    keep = pltpu.make_async_copy(send.at[chip], got.at[7], local_sem.at[0])
+    for d in ORDER:
+        plane, moved, group = nearest(d, y)
+
+        def dispatch(j, carry):
+            dx = (j + 1 - group % 2) % 4
+            slot = group // 2 * chunk + (1 - group % 2) * 4 + j
+
+            @pl.when(jnp.logical_or(group != 0, dx != 0))
+            def _():
+                remote(
+                    send.at[place.at(d, dx)], got.at[slot], send_sem, got_sem.at[group // 2],
+                    ctx=place.at(moved, dx) * 2 + core, ch=plane,
+                ).start()
+
+            return carry
+
+        lax.fori_loop(0, 4, dispatch, 0)
+    home = place.at(-shift_of(y), 0)
+    keep = pltpu.make_async_copy(send.at[home], got.at[7], local_sem.at[0])
     keep.start()
-    keep_back = pltpu.make_async_copy(summed.at[7], back.at[chip], local_sem.at[1])
+    keep_back = pltpu.make_async_copy(summed.at[7], back.at[home], local_sem.at[1])
     hi, lo = gates_of(normed, router_t[...], here[...])
     quarters.wait_send()
     whole_back.wait_send()
+
+    for side in range(2):
+        pl.when(y != 1 + 2 * side)(lambda: act(step_along_y(side), "wait_send"))
+        pl.when(y == 1 + 2 * side)(lambda: act(stays(side), "wait"))
+    pl.when(y % 2 == 0)(lambda: act(whole_weights(), "wait"))
+
+    @pl.when(y % 2 == 1)
+    def _():
+        three = pl.ds(0, 3 * wide), pl.ds(0, 3 * deep)
+        remote(own_up.at[three[0]], up_ref.at[three[0]], ys_sem.at[0, 0], yr_sem.at[0], ch=0).wait_recv()
+        remote(own_down.at[three[1]], down_ref.at[three[1]], ys_sem.at[0, 1], yr_sem.at[1], ch=0).wait_recv()
 
     def mlp(block):
         x = block.reshape(rows, block.shape[-1])
@@ -321,11 +419,17 @@
         total = own[...].reshape(chunk, CAP, -1) + twin_part[slots].astype(f32)
         summed[slots] = total.astype(bf16)
 
-        def give_back(slot, dz, dx):
-            to = place.at(-dz, -dx)
-            remote(summed.at[slot], back.at[chip], rs_sem, back_sem, ctx=to * 2 + core).start()
-
-        each(q, give_back)
+        for odd_group in range(2):
+            moved, sender = came_from(q, odd_group, y)
+
+            def give_back(j, carry):
+                dx = (j + 1 - odd_group) % 4
+                slot = q * chunk + (1 - odd_group) * 4 + j
+                to = place.at(-moved, -dx) * 2 + core
+                remote(summed.at[slot], back.at[home], rs_sem, back_sem, ctx=to, ch=sender).start()
+                return carry
+
+            lax.fori_loop(0, 3 if q == 0 and odd_group == 0 else 4, give_back, 0)
         if q == 0:
             keep_back.start()
         share.wait_send()
@@ -369,6 +473,7 @@
     experts = router.shape[1]
     width = norm_gain.shape[0]
     rows = tok_dev // groups
+    hidden = w_up.shape[2]
     shape = jax.ShapeDtypeStruct
     far = (*dft_constants(shards, tok_dev, chans), w_up[0], w_down[0])
     blocks = (experts, CAP, width)
@@ -393,9 +498,13 @@
         + [vmem(blocks, bf16)] * 6
         + [vmem((groups, rows, ch_dev), bf16)] * 2
         + [vmem((rows, width), f32)]
+        + [vmem((2, width // 4, hidden), bf16), vmem((2, hidden // 4, width), bf16)]
+        + [vmem((width, hidden), bf16), vmem((hidden, width), bf16)]
         + [dma((9,)), dma((3,)), dma((4,)), dma, dma, dma]
         + [dma((4,))] * 5
-        + [dma, dma, dma((3,)), dma((3,))],
+        + [dma, dma, dma((3,)), dma((3,))]
+        + [dma((2, 2))] * 3
+        + [dma((2,))] * 2,
         compiler_params=pltpu.CompilerParams(collective_id=0, has_side_effects=True),
     )(signal, taps, skip[None, :], norm_gain[None, :], router.T, routes.T, gate_v, *far)
     return (mixed, moe_out)

time: 104 us -> 115 us (1.11)
  Pallas kernels: 101 us -> 111 us
    pallas_call x1, Pallas kernels: 101 us -> 111 us  [body(): pl.pallas_call(layer_kernel, out_shape=(local, local), in_specs=[here] *...]
where the time goes in v5:
time: 115 us; the launch traced here: 114 us
  Pallas kernels  111 us (97%)
  local copies, waits for them, and re-layouts  2.42 us (2%)
    pallas_call x1, Pallas kernels, body(): pl.pallas_call(layer_kernel, out_shape=(local, local), in_specs=[here] *...  111 us
    unnamed x4, local copies, waits for them, and re-layouts  2.42 us

profile of v5, /device:TPU:1, one launch (start us, length us, event | category | flops | bytes accessed | tf_op | source)
XLA Modules:
  0.0 114.4 jit_solution(160455427950172038)
XLA Ops:
  0.6 111.3 %shard_map.158 = (bf16[512,256]{1,0:T(8,128)(2,1)}, bf16[512,256]{1,0:T(8,128)(2,1)}) custom-call(bf16[512,256]{1,0:T(8,128)(2,1)} %signal.1, f32[512,256]{1,0:T(8,128)} %taps.1, f32[1,256]{1,0:T(1,128)} %bitcast.10, f32[1,1024]{1,0:T(1,128)} %bitcast.9, f32[32,1024]{1,0:T(8,128)} %bitcast.8, s32[2,128]{1,0:T(2,128)} %bitcast.11, bf16[512,256]{1,0:T(8,128)(2,1)} %gate_hbm.1, ...), custom_call_target="tpu_custom_call" | custom-call | tf_op jit(solution)/shard_map/pallas_call | solution.py:485
  112.0 0.0 copy-start
  112.0 1.7 %copy.19 = bf16[512,256]{1,0:T(8,128)(2,1)} copy(bf16[512,256]{1,0:T(8,128)(2,1)} %get-tuple-element.4) | data formatting | bytes 524288
  113.7 0.0 copy-done
  113.7 0.7 copy.20
Async XLA Ops:
  112.0 1.7 %copy-start = (bf16[512,256]{1,0:T(8,128)(2,1)S(1)}, bf16[512,256]{1,0:T(8,128)(2,1)}, u32[]{:S(2)}) copy-start(bf16[512,256]{1,0:T(8,128)(2,1)} %get-tuple-element.5) | copy-start | bytes 786436

commit v6 on v4

--- a/solution.py
+++ b/solution.py
@@ -201,40 +201,42 @@
         lax.fori_loop(0, 3 if q == 0 and half == 1 else 4, one, 0)
 
 
-def split(refs, far, outs, conv, moe, sems):
+def split(refs, counts):
     refs = list(refs)
-    cut = [refs[:far], refs[far : far + outs]]
-    rest = refs[far + outs :]
-    first = rest[:conv]
-    cut.append((first[: far + 1], *first[far + 1 :]))
-    cut.append(rest[conv : conv + moe])
-    cut.append(rest[conv + moe :])
-    return cut
+    return [[refs.pop(0) for _ in range(count)] for count in counts]
+
+
+def publish_kernel(a_ref, b_ref, a_out, b_out):
+    a_out[...] = a_ref[...]
+    b_out[...] = b_ref[...]
 
 
 def layer_kernel(
-    signal, taps, skip, gain, router_t, routes_t, gate_hbm, *rest
+    skip, gain, routes_t, *rest
 ):
     place = Place()
     me, core, chip, y = place.me, place.core, place.chip, place.y
     (
         far, (mixed_out, out),
-        (near, packed, fields, re_ref, im_ref, conv_out, conv_in, mixed, full),
-        (send, here, got, twin_got, part, twin_part, summed, back, moe, landed, own),
-        (far_sem, local_sem, conv_sem, xs_sem, xr_sem, send_sem, got_sem, fs_sem, fr_sem, ps_sem, pr_sem,
+        near, (packed, fields, re_ref, im_ref, conv_out, conv_in, mixed, full),
+        (send, here, got, summed, back, moe, landed, ups, downs),
+        (far_sem, local_sem, conv_sem, xs_sem, xr_sem, send_sem, got_sem, ws_sem, wr_sem,
          rs_sem, back_sem, ms_sem, mr_sem),
-    ) = split(rest, 8, 2, 17, 11, 15)
-    shards, width_ch = 64, signal.shape[1]
+    ) = split(rest, (12, 2, 10, 8, 9, 13))
+    shards, width_ch = 64, near[0].shape[1]
     chans = width_ch // shards
     ready = greet(place, shards, 4)
-    fetches = [
-        pltpu.make_async_copy(a, b, far_sem.at[i]) for i, (a, b) in enumerate(zip((gate_hbm, *far), near))
-    ]
+    near = (*near, ups.at[0], downs.at[0])
+    fetches = [pltpu.make_async_copy(a, b, far_sem.at[i]) for i, (a, b) in enumerate(zip(far, near))]
     for fetch in fetches:
         fetch.start()
-    gate, tables, up_ref, down_ref = near[0], near[1:7], near[7], near[8]
+    signal, taps, gate, router_t, tables = near[0], near[1], near[2], near[3], near[4:10]
+    fetches[0].wait()
+    fetches[1].wait()
     packed[...] = pack(signal[...], taps[...], shards, 2 * chans).reshape(packed.shape).astype(bf16)
     here[...] = slots_of(routes_t[...], router_t.shape[0])
+    for fetch in fetches[2:]:
+        fetch.wait()
     ready()
 
     def spread_out(source, target, ss, rs):
@@ -254,9 +256,13 @@
         stay.wait()
         return whole
 
+    swaps = [
+        remote(both.at[0], both.at[1], ws_sem.at[i], wr_sem.at[i], ctx=place.twin)
+        for i, both in enumerate((ups, downs))
+    ]
     whole = spread_out(packed, fields, conv_sem.at[0], conv_sem.at[1])
-    for fetch in fetches:
-        fetch.wait()
+    for swap in swaps:
+        swap.start()
     data = fields[...].astype(f32).reshape(shards * 2 * chans, -1).astype(bf16)
     total = convolve(data, tables, re_ref, im_ref, shards, chans)
     conv_out[...] = total.reshape(conv_out.shape).astype(bf16)
@@ -299,27 +305,21 @@
     quarters.wait_send()
     whole_back.wait_send()
 
-    def mlp(block):
-        x = block.reshape(rows, block.shape[-1])
-        hidden = jax.nn.gelu(dot(x, up_ref[...]), approximate=True).astype(bf16)
-        return dot(hidden, down_ref[...])
-
+    for swap in swaps:
+        swap.wait()
     for q in range(4):
         slots = pl.ds(q * chunk, chunk)
         came = pl.ds(q * chunk, 7) if q == 0 else slots
         remote(send.at[came], got.at[came], send_sem, got_sem.at[q], ctx=me).wait_recv()
         if q == 0:
             keep.wait()
-        share = remote(got.at[slots], twin_got.at[slots], fs_sem.at[q], fr_sem.at[q], ctx=place.twin)
-        share.start()
-        own[...] = mlp(got[slots])
-        share.wait_recv()
-        part[slots] = mlp(twin_got[slots]).astype(bf16).reshape(chunk, CAP, -1)
-        give = remote(part.at[slots], twin_part.at[slots], ps_sem.at[q], pr_sem.at[q], ctx=place.twin)
-        give.start()
-        give.wait_recv()
-        total = own[...].reshape(chunk, CAP, -1) + twin_part[slots].astype(f32)
-        summed[slots] = total.astype(bf16)
+        x = got[slots].reshape(rows, -1)
+        total = None
+        for half in range(2):
+            hidden = jax.nn.gelu(dot(x, ups[half]), approximate=True).astype(bf16)
+            part = dot(hidden, downs[half])
+            total = part if half == 0 else total + part
+        summed[slots] = total.astype(bf16).reshape(chunk, CAP, -1)
 
         def give_back(slot, dz, dx):
             to = place.at(-dz, -dx)
@@ -328,8 +328,6 @@
         each(q, give_back)
         if q == 0:
             keep_back.start()
-        share.wait_send()
-        give.wait_send()
     keep_back.wait()
     others = pl.ds(0, 31)
     remote(summed.at[others], back.at[others], rs_sem, back_sem, ctx=me).wait_recv()
@@ -370,35 +368,44 @@
     width = norm_gain.shape[0]
     rows = tok_dev // groups
     shape = jax.ShapeDtypeStruct
-    far = (*dft_constants(shards, tok_dev, chans), w_up[0], w_down[0])
+    far = (
+        signal, taps, gate_v, router.T, *dft_constants(shards, tok_dev, chans), w_up[0], w_down[0],
+    )
+    hidden = w_up.shape[2]
     blocks = (experts, CAP, width)
     dma = pltpu.SemaphoreType.DMA
     vmem = pltpu.VMEM
     here = pl.BlockSpec(memory_space=vmem)
     there = pl.BlockSpec(memory_space=pl.ANY)
     local = shape((tok_dev, ch_dev), bf16)
-    mixed, moe_out = pl.pallas_call(
+    results = pl.pallas_call(
         layer_kernel,
         out_shape=(local, local),
-        in_specs=[here] * 6 + [there] * (1 + len(far)),
+        in_specs=[here] * 3 + [there] * len(far),
         out_specs=(here, here),
-        scratch_shapes=[vmem(gate_v.shape, gate_v.dtype)]
-        + [vmem(a.shape, a.dtype) for a in far]
+        scratch_shapes=[vmem(a.shape, a.dtype) for a in far[:-2]]
         + [vmem((shards, 2 * chans, tok_dev), bf16)] * 2
         + [vmem((2 * chans * shards, tok_dev), bf16)] * 2
         + [vmem((shards, 2 * chans, tok_dev // 2), bf16)] * 2
         + [vmem((groups, rows, ch_dev), bf16)] * 2
         + [vmem(blocks, bf16)]
         + [vmem((experts * CAP, rows), bf16)]
-        + [vmem(blocks, bf16)] * 6
+        + [vmem(blocks, bf16)] * 3
         + [vmem((groups, rows, ch_dev), bf16)] * 2
-        + [vmem((rows, width), f32)]
-        + [dma((9,)), dma((3,)), dma((4,)), dma, dma, dma]
-        + [dma((4,))] * 5
+        + [vmem((2, width, hidden), bf16), vmem((2, hidden, width), bf16)]
+        + [dma((12,)), dma((3,)), dma((4,)), dma, dma, dma]
+        + [dma((4,)), dma((2,)), dma((2,))]
         + [dma, dma, dma((3,)), dma((3,))],
         compiler_params=pltpu.CompilerParams(collective_id=0, has_side_effects=True),
-    )(signal, taps, skip[None, :], norm_gain[None, :], router.T, routes.T, gate_v, *far)
-    return (mixed, moe_out)
+    )(skip[None, :], norm_gain[None, :], routes.T, *far)
+    return tuple(
+        pl.pallas_call(
+            publish_kernel,
+            out_shape=(local, local),
+            in_specs=[here] * 2,
+            out_specs=(here, here),
+        )(*results)
+    )
 
 
 def solution(mesh):

time: 104 us -> 103 us (level)
  local copies, waits for them, and re-layouts: 2.42 us -> 0 us
    unnamed x4 -> x0, local copies, waits for them, and re-layouts: 2.42 us -> none
    pallas_call x0 -> x1, Pallas kernels: none -> 1.84 us  [body(): pl.pallas_call(publish_kernel, out_shape=(local, local), in_specs=[here]...]
where the time goes in v6:
time: 103 us
  Pallas kernels  102 us (99%)
    pallas_call x1, Pallas kernels, body(): pl.pallas_call(layer_kernel, out_shape=(local, local), in_specs=[here] *...  100 us

profile of v6, /device:TPU:1, one launch (start us, length us, event | category | flops | bytes accessed | tf_op | source)
XLA Modules:
  0.0 102.5 jit_solution(13787295331650871139)
XLA Ops:
  0.6 100.1 %shard_map.158 = (bf16[512,256]{1,0:T(8,128)(2,1)}, bf16[512,256]{1,0:T(8,128)(2,1)}) custom-call(f32[1,256]{1,0:T(1,128)} %bitcast.10, f32[1,1024]{1,0:T(1,128)} %bitcast.9, s32[2,128]{1,0:T(2,128)} %bitcast.11, bf16[512,256]{1,0:T(8,128)(2,1)} %rest_0_.1, f32[512,256]{1,0:T(8,128)} %rest_1_.1, bf16[512,256]{1,0:T(8,128)(2,1)} %rest_2_.1, ...), custom_call_target="tpu_custom_call" | custom-call | tf_op jit(solution)/shard_map/pallas_call | solution.py:381
  100.7 1.8 %shard_map.159 = (bf16[512,256]{1,0:T(8,128)(2,1)}, bf16[512,256]{1,0:T(8,128)(2,1)}) custom-call(bf16[512,256]{1,0:T(8,128)(2,1)} %get-tuple-element.4.a_ref, bf16[512,256]{1,0:T(8,128)(2,1)} %get-tuple-element.5.b_ref), custom_call_target="tpu_custom_call" | custom-call | tf_op jit(solution)/shard_map/pallas_call | solution.py:402

commit v7 on v6

--- a/solution.py
+++ b/solution.py
@@ -121,27 +121,6 @@
     return (x * scale * gain).astype(bf16)
 
 
-def gates_of(normed, router_t, here):
-    count = normed.shape[0]
-    experts = router_t.shape[0]
-    slots = experts * CAP
-    logits = lax.dot_general(
-        router_t,
-        normed.astype(f32),
-        (((1,), (1,)), ((), ())),
-        precision=lax.Precision.HIGHEST,
-        preferred_element_type=f32,
-    )
-    gates = jax.nn.sigmoid(logits)
-    high = gates.astype(bf16)
-    low = (gates - high.astype(f32)).astype(bf16)
-    spread = one_hot(iota((slots, experts), 0) // CAP == iota((slots, experts), 1))
-    turn = one_hot(iota((count, count), 0) == iota((count, count), 1))
-    chosen = here > 0.5
-    parts = (jnp.where(chosen, dot(spread, part), 0.0).astype(bf16) for part in (high, low))
-    return tuple(contract(turn, part, 1, 1).astype(bf16) for part in parts)
-
-
 def remote(src, dst, send_sem, recv_sem, **where):
     return pltpu.make_async_remote_copy(
         src_ref=src,
@@ -211,21 +190,19 @@
     b_out[...] = b_ref[...]
 
 
-def layer_kernel(
-    skip, gain, routes_t, *rest
-):
+def layer_kernel(skip, gain, routes_t, *rest):
     place = Place()
     me, core, chip, y = place.me, place.core, place.chip, place.y
     (
         far, (mixed_out, out),
-        near, (packed, fields, re_ref, im_ref, conv_out, conv_in, mixed, full),
-        (send, here, got, summed, back, moe, landed, ups, downs),
-        (far_sem, local_sem, conv_sem, xs_sem, xr_sem, send_sem, got_sem, ws_sem, wr_sem,
-         rs_sem, back_sem, ms_sem, mr_sem),
-    ) = split(rest, (12, 2, 10, 8, 9, 13))
+        near, (packed, fields, re_ref, im_ref, conv_out, conv_in, routes_all),
+        (send, here, got, summed, back, ups, downs),
+        (far_sem, local_sem, conv_sem, xs_sem, xr_sem, send_sem, got_sem, ws_sem, wr_sem, rs_sem, back_sem),
+    ) = split(rest, (12, 2, 10, 7, 7, 11))
     shards, width_ch = 64, near[0].shape[1]
     chans = width_ch // shards
-    ready = greet(place, shards, 4)
+    chips, groups, chunk = 32, 4, 8
+    ready = greet(place, shards, groups)
     near = (*near, ups.at[0], downs.at[0])
     fetches = [pltpu.make_async_copy(a, b, far_sem.at[i]) for i, (a, b) in enumerate(zip(far, near))]
     for fetch in fetches:
@@ -234,12 +211,12 @@
     fetches[0].wait()
     fetches[1].wait()
     packed[...] = pack(signal[...], taps[...], shards, 2 * chans).reshape(packed.shape).astype(bf16)
-    here[...] = slots_of(routes_t[...], router_t.shape[0])
+    routes_all[y] = routes_t[...]
     for fetch in fetches[2:]:
         fetch.wait()
     ready()
 
-    def spread_out(source, target, ss, rs):
+    def spread_out(source, target, ss, rs, meanwhile):
         def both(to):
             for side in range(2):
                 where = to * 2 + side
@@ -250,24 +227,37 @@
         remote(source.at[place.twin], target.at[me], ss, rs, ctx=place.twin).start()
         stay = pltpu.make_async_copy(source.at[me], target.at[me], local_sem.at[2])
         stay.start()
+        meanwhile()
         most = pl.ds(0, shards - 1)
         whole = remote(source.at[most], target.at[most], ss, rs, ctx=place.twin)
         whole.wait_recv()
         stay.wait()
         return whole
 
+    tells = [
+        remote(routes_t, routes_all.at[y], xs_sem.at[dy - 1], xr_sem.at[dy - 1], ch=(y + dy) % groups)
+        for dy in range(1, groups)
+    ]
+
+    def all_slots():
+        for tell in tells:
+            tell.wait()
+        for k in range(groups):
+            here[k] = slots_of(routes_all[k], chips)
+
     swaps = [
         remote(both.at[0], both.at[1], ws_sem.at[i], wr_sem.at[i], ctx=place.twin)
         for i, both in enumerate((ups, downs))
     ]
-    whole = spread_out(packed, fields, conv_sem.at[0], conv_sem.at[1])
+    for tell in tells:
+        tell.start()
+    whole = spread_out(packed, fields, conv_sem.at[0], conv_sem.at[1], all_slots)
     for swap in swaps:
         swap.start()
     data = fields[...].astype(f32).reshape(shards * 2 * chans, -1).astype(bf16)
     total = convolve(data, tables, re_ref, im_ref, shards, chans)
     conv_out[...] = total.reshape(conv_out.shape).astype(bf16)
-    whole_back = spread_out(conv_out, conv_in, conv_sem.at[2], conv_sem.at[3])
-    whole.wait_send()
+    whole_back = spread_out(conv_out, conv_in, conv_sem.at[2], conv_sem.at[3], lambda: None)
     data = conv_in[...].astype(f32).reshape(shards * 2 * chans, -1).astype(bf16)
     for side in range(2):
         conv = unpack(data, side, 2 * chans)
@@ -276,87 +266,78 @@
         sig = signal[span, :].astype(f32)
         value = (gate[span, :].astype(f32) * (conv + skip[...] * sig)).astype(bf16)
         mixed_out[span, :] = value
-        for k in range(2 * side, 2 * side + 2):
-            mixed[k] = value[(k % 2) * (count // 2) : (k % 2 + 1) * (count // 2)]
-
-            @pl.when(y != k)
-            def _():
-                remote(mixed.at[k], full.at[y], xs_sem, xr_sem, ch=k).start()
-
-    full[y] = mixed[y]
-    trio = pl.ds(0, 3)
-    quarters = remote(mixed.at[trio], full.at[trio], xs_sem, xr_sem, ch=(y + 1) % 4)
-    quarters.wait_recv()
-    normed = normalize(jnp.concatenate([full[k] for k in range(4)], axis=1).astype(f32), gain[...])
-    send[...] = dot(here[...], normed).astype(bf16).reshape(send.shape)
-    chunk = 8
-    rows = chunk * CAP
+        for part in range(2):
+            k = 2 * side + part
+            rows = value[part * (count // 2) : (part + 1) * (count // 2)]
+            send[k * chips : (k + 1) * chips] = dot(here[k], rows).astype(bf16).reshape(chips, CAP, width_ch)
+
     for q in range(4):
 
         def dispatch(slot, dz, dx):
             to = place.at(dz, dx)
-            remote(send.at[to], got.at[slot], send_sem, got_sem.at[q], ctx=to * 2 + core).start()
+            for k in range(groups):
+                remote(
+                    send.at[k * chips + to], got.at[y * chips + slot], send_sem, got_sem.at[q],
+                    ctx=to * 2 + core, ch=k,
+                ).start()
 
         each(q, dispatch)
-    keep = pltpu.make_async_copy(send.at[chip], got.at[7], local_sem.at[0])
+        if q == 0:
+            for dy in range(1, groups):
+                k = (y + dy) % groups
+                remote(
+                    send.at[k * chips + chip], got.at[y * chips + 7], send_sem, got_sem.at[0], ch=k
+                ).start()
+    mine = y * chips + chip
+    keep = pltpu.make_async_copy(send.at[mine], got.at[y * chips + 7], local_sem.at[0])
     keep.start()
-    keep_back = pltpu.make_async_copy(summed.at[7], back.at[chip], local_sem.at[1])
-    hi, lo = gates_of(normed, router_t[...], here[...])
-    quarters.wait_send()
+    keep_back = pltpu.make_async_copy(summed.at[y * chips + 7], back.at[mine], local_sem.at[1])
+    whole.wait_send()
     whole_back.wait_send()
-
     for swap in swaps:
         swap.wait()
+    column = router_t[pl.ds(chip, 1), :]
     for q in range(4):
-        slots = pl.ds(q * chunk, chunk)
-        came = pl.ds(q * chunk, 7) if q == 0 else slots
+        came = pl.ds(0, groups * chunk - (q == 0))
         remote(send.at[came], got.at[came], send_sem, got_sem.at[q], ctx=me).wait_recv()
         if q == 0:
             keep.wait()
-        x = got[slots].reshape(rows, -1)
+        slices = [got[k * chips + q * chunk : k * chips + (q + 1) * chunk] for k in range(groups)]
+        x = jnp.concatenate([piece.reshape(chunk * CAP, width_ch) for piece in slices], axis=1)
+        normed = normalize(x.astype(f32), gain[...])
+        logit = jnp.sum(normed.astype(f32) * column, axis=-1, keepdims=True)
         total = None
         for half in range(2):
-            hidden = jax.nn.gelu(dot(x, ups[half]), approximate=True).astype(bf16)
+            hidden = jax.nn.gelu(dot(normed, ups[half]), approximate=True).astype(bf16)
             part = dot(hidden, downs[half])
             total = part if half == 0 else total + part
-        summed[slots] = total.astype(bf16).reshape(chunk, CAP, -1)
+        total = (jax.nn.sigmoid(logit) * total).astype(bf16)
+        for k in range(groups):
+            piece = total[:, k * width_ch : (k + 1) * width_ch].reshape(chunk, CAP, width_ch)
+            summed[k * chips + q * chunk : k * chips + (q + 1) * chunk] = piece
 
         def give_back(slot, dz, dx):
-            to = place.at(-dz, -dx)
-            remote(summed.at[slot], back.at[chip], rs_sem, back_sem, ctx=to * 2 + core).start()
+            to = place.at(-dz, -dx) * 2 + core
+            for k in range(groups):
+                remote(
+                    summed.at[k * chips + slot], back.at[mine], rs_sem, back_sem, ctx=to, ch=k
+                ).start()
 
         each(q, give_back)
         if q == 0:
+            for dy in range(1, groups):
+                k = (y + dy) % groups
+                remote(summed.at[k * chips + 7], back.at[mine], rs_sem, back_sem, ch=k).start()
             keep_back.start()
     keep_back.wait()
-    others = pl.ds(0, 31)
+    others = pl.ds(0, groups * chips - 1)
     remote(summed.at[others], back.at[others], rs_sem, back_sem, ctx=me).wait_recv()
-    gathered = back[...].reshape(32 * CAP, -1)
-    result = (dot(hi, gathered) + dot(lo, gathered)).astype(bf16)
-    width = moe.shape[-1]
-    for k in range(4):
-        moe[k] = result[:, k * width : (k + 1) * width]
-    copies = []
-    for dy in range(1, 4):
-        to = (y + dy) % 4
-        copies.append(remote(moe.at[to], landed.at[y], ms_sem.at[dy - 1], mr_sem.at[dy - 1], ch=to))
-        copies[-1].start()
-    landed[y] = moe[y]
-    for copy in copies:
-        copy.wait()
-    out[...] = landed[...].reshape(out.shape)
+    for k in range(groups):
+        slots = back[k * chips : (k + 1) * chips].reshape(chips * CAP, width_ch)
+        rows = contract(here[k], slots, 0, 0).astype(bf16)
+        out[k * rows.shape[0] : (k + 1) * rows.shape[0], :] = rows
     remote(send.at[others], got.at[others], send_sem, got_sem.at[0], ctx=me).wait_send()
     remote(summed.at[others], back.at[others], rs_sem, back_sem, ctx=me).wait_send()
-
-
-def call(kernel, out_shape, *args, scratch=()):
-    return pl.pallas_call(
-        kernel,
-        out_shape=out_shape,
-        in_specs=[pl.BlockSpec(memory_space=pltpu.VMEM)] * len(args),
-        out_specs=jax.tree.map(lambda _: pl.BlockSpec(memory_space=pltpu.VMEM), out_shape),
-        scratch_shapes=list(scratch),
-    )(*args)
 
 
 def body(signal, gate_v, taps, skip, norm_gain, router, w_up, w_down, routes):
@@ -372,7 +353,7 @@
         signal, taps, gate_v, router.T, *dft_constants(shards, tok_dev, chans), w_up[0], w_down[0],
     )
     hidden = w_up.shape[2]
-    blocks = (experts, CAP, width)
+    blocks = (groups * experts, CAP, ch_dev)
     dma = pltpu.SemaphoreType.DMA
     vmem = pltpu.VMEM
     here = pl.BlockSpec(memory_space=vmem)
@@ -387,15 +368,13 @@
         + [vmem((shards, 2 * chans, tok_dev), bf16)] * 2
         + [vmem((2 * chans * shards, tok_dev), bf16)] * 2
         + [vmem((shards, 2 * chans, tok_dev // 2), bf16)] * 2
-        + [vmem((groups, rows, ch_dev), bf16)] * 2
+        + [vmem((groups, 2, rows), routes.dtype)]
         + [vmem(blocks, bf16)]
-        + [vmem((experts * CAP, rows), bf16)]
+        + [vmem((groups, experts * CAP, rows), bf16)]
         + [vmem(blocks, bf16)] * 3
-        + [vmem((groups, rows, ch_dev), bf16)] * 2
         + [vmem((2, width, hidden), bf16), vmem((2, hidden, width), bf16)]
-        + [dma((12,)), dma((3,)), dma((4,)), dma, dma, dma]
-        + [dma((4,)), dma((2,)), dma((2,))]
-        + [dma, dma, dma((3,)), dma((3,))],
+        + [dma((12,)), dma((3,)), dma((4,)), dma((3,)), dma((3,)), dma]
+        + [dma((4,)), dma((2,)), dma((2,)), dma, dma],
         compiler_params=pltpu.CompilerParams(collective_id=0, has_side_effects=True),
     )(skip[None, :], norm_gain[None, :], routes.T, *far)
     return tuple(

time: 103 us -> 94.5 us (0.917)
  Pallas kernels: 102 us -> 93.7 us
    pallas_call x1, Pallas kernels: 100 us -> 91.9 us  [body(): pl.pallas_call(layer_kernel, out_shape=(local, local), in_specs=[here] *...]
where the time goes in v7:
time: 94.5 us; the launch traced here: 94.3 us
  Pallas kernels  93.7 us (99%)
    pallas_call x1, Pallas kernels, body(): pl.pallas_call(layer_kernel, out_shape=(local, local), in_specs=[here] *...  91.9 us

profile of v7, /device:TPU:1, one launch (start us, length us, event | category | flops | bytes accessed | tf_op | source)
XLA Modules:
  0.0 94.3 jit_solution(12616425224824016174)
XLA Ops:
  0.6 91.9 %shard_map.158 = (bf16[512,256]{1,0:T(8,128)(2,1)}, bf16[512,256]{1,0:T(8,128)(2,1)}) custom-call(f32[1,256]{1,0:T(1,128)} %bitcast.10, f32[1,1024]{1,0:T(1,128)} %bitcast.9, s32[2,128]{1,0:T(2,128)} %bitcast.11, bf16[512,256]{1,0:T(8,128)(2,1)} %rest_0_.1, f32[512,256]{1,0:T(8,128)} %rest_1_.1, bf16[512,256]{1,0:T(8,128)(2,1)} %rest_2_.1, ...), custom_call_target="tpu_custom_call" | custom-call | tf_op jit(solution)/shard_map/pallas_call | solution.py:362
  92.5 1.8 %shard_map.159 = (bf16[512,256]{1,0:T(8,128)(2,1)}, bf16[512,256]{1,0:T(8,128)(2,1)}) custom-call(bf16[512,256]{1,0:T(8,128)(2,1)} %get-tuple-element.4.a_ref, bf16[512,256]{1,0:T(8,128)(2,1)} %get-tuple-element.5.b_ref), custom_call_target="tpu_custom_call" | custom-call | tf_op jit(solution)/shard_map/pallas_call | solution.py:381

commit v8 on v7

--- a/solution.py
+++ b/solution.py
@@ -65,9 +65,8 @@
 
 
 def convolve(data, tables, re_ref, im_ref, shards, chans):
-    first, tr, ti, cos, sin, last = (table[...] for table in tables)
+    first, tr, ti, cos, sin = (table[...] for table in tables[:5])
     fields = 2 * chans
-    tok = data.shape[1]
     lane = iota(first.shape, 1) % fields
     for field in range(fields):
         g = dot(jnp.where(lane == field, first, jnp.zeros_like(first)), data)
@@ -83,16 +82,25 @@
     p_im = (x_re[:half] * x_im[half:] + x_im[:half] * x_re[half:]).astype(bf16)
     g_re = dot(p_re, cos) - dot(p_im, sin)
     g_im = dot(p_im, cos) + dot(p_re, sin)
-    row = iota(last.shape, 0) % fields
-    total = jnp.zeros((shards * fields, tok // 2), f32)
+    pairs = []
     for chan in range(chans):
         rows = slice(chan * shards, (chan + 1) * shards)
         a = (g_re[rows] * tr + g_im[rows] * ti).astype(bf16)
         b = (g_im[rows] * tr - g_re[rows] * ti).astype(bf16)
-        both = jnp.concatenate([a, b], axis=0)
-        for side in range(2):
-            table = jnp.where(row == side * chans + chan, last, jnp.zeros_like(last))
-            total += dot(table, both[:, side * (tok // 2) : (side + 1) * (tok // 2)])
+        pairs.append(jnp.concatenate([a, b], axis=0))
+    return pairs
+
+
+def last_step(pairs, last, side):
+    chans = len(pairs)
+    row = iota(last.shape, 0) % (2 * chans)
+    count = pairs[0].shape[1] // 4
+    total = jnp.zeros((last.shape[0], count), f32)
+    for chan, pair in enumerate(pairs):
+        for part in range(2):
+            table = jnp.where(row == part * chans + chan, last, jnp.zeros_like(last))
+            start = (2 * side + part) * count
+            total += dot(table, pair[:, start : start + count])
     return total
 
 
@@ -216,7 +224,7 @@
         fetch.wait()
     ready()
 
-    def spread_out(source, target, ss, rs, meanwhile):
+    def spread_out(source, target, ss, rs, stay_sem):
         def both(to):
             for side in range(2):
                 where = to * 2 + side
@@ -225,14 +233,16 @@
         for q in range(4):
             each(q, lambda slot, dz, dx: both(place.at(dz, dx)))
         remote(source.at[place.twin], target.at[me], ss, rs, ctx=place.twin).start()
-        stay = pltpu.make_async_copy(source.at[me], target.at[me], local_sem.at[2])
+        stay = pltpu.make_async_copy(source.at[me], target.at[me], stay_sem)
         stay.start()
-        meanwhile()
         most = pl.ds(0, shards - 1)
         whole = remote(source.at[most], target.at[most], ss, rs, ctx=place.twin)
-        whole.wait_recv()
-        stay.wait()
-        return whole
+
+        def arrive():
+            whole.wait_recv()
+            stay.wait()
+
+        return whole, arrive
 
     tells = [
         remote(routes_t, routes_all.at[y], xs_sem.at[dy - 1], xr_sem.at[dy - 1], ch=(y + dy) % groups)
@@ -251,49 +261,62 @@
     ]
     for tell in tells:
         tell.start()
-    whole = spread_out(packed, fields, conv_sem.at[0], conv_sem.at[1], all_slots)
+    whole, arrive = spread_out(packed, fields, conv_sem.at[0], conv_sem.at[1], local_sem.at[2])
+    all_slots()
+    arrive()
     for swap in swaps:
         swap.start()
     data = fields[...].astype(f32).reshape(shards * 2 * chans, -1).astype(bf16)
-    total = convolve(data, tables, re_ref, im_ref, shards, chans)
-    conv_out[...] = total.reshape(conv_out.shape).astype(bf16)
-    whole_back = spread_out(conv_out, conv_in, conv_sem.at[2], conv_sem.at[3], lambda: None)
-    data = conv_in[...].astype(f32).reshape(shards * 2 * chans, -1).astype(bf16)
+    pairs = convolve(data, tables, re_ref, im_ref, shards, chans)
+    returns = []
     for side in range(2):
-        conv = unpack(data, side, 2 * chans)
-        count = conv.shape[0]
-        span = slice(side * count, (side + 1) * count)
-        sig = signal[span, :].astype(f32)
-        value = (gate[span, :].astype(f32) * (conv + skip[...] * sig)).astype(bf16)
-        mixed_out[span, :] = value
+        conv_out[side] = last_step(pairs, tables[5][...], side).reshape(conv_out.shape[1:]).astype(bf16)
+        returns.append(
+            spread_out(
+                conv_out.at[side], conv_in.at[side], conv_sem.at[2 + 2 * side], conv_sem.at[3 + 2 * side],
+                local_sem.at[3 + side],
+            )
+        )
+    mine = y * chips + chip
+    keep = pltpu.make_async_copy(send.at[mine], got.at[y * chips + 7], local_sem.at[0])
+    for side in range(2):
+        returns[side][1]()
+        data = conv_in[side].astype(f32).reshape(shards * 2 * chans, -1).astype(bf16)
         for part in range(2):
             k = 2 * side + part
-            rows = value[part * (count // 2) : (part + 1) * (count // 2)]
-            send[k * chips : (k + 1) * chips] = dot(here[k], rows).astype(bf16).reshape(chips, CAP, width_ch)
-
-    for q in range(4):
-
-        def dispatch(slot, dz, dx):
-            to = place.at(dz, dx)
-            for k in range(groups):
-                remote(
-                    send.at[k * chips + to], got.at[y * chips + slot], send_sem, got_sem.at[q],
-                    ctx=to * 2 + core, ch=k,
-                ).start()
-
-        each(q, dispatch)
-        if q == 0:
-            for dy in range(1, groups):
-                k = (y + dy) % groups
-                remote(
-                    send.at[k * chips + chip], got.at[y * chips + 7], send_sem, got_sem.at[0], ch=k
-                ).start()
-    mine = y * chips + chip
-    keep = pltpu.make_async_copy(send.at[mine], got.at[y * chips + 7], local_sem.at[0])
-    keep.start()
+            conv = unpack(data, part, 2 * chans)
+            count = conv.shape[0]
+            span = slice(k * count, (k + 1) * count)
+            sig = signal[span, :].astype(f32)
+            value = (gate[span, :].astype(f32) * (conv + skip[...] * sig)).astype(bf16)
+            mixed_out[span, :] = value
+            send[k * chips : (k + 1) * chips] = dot(here[k], value).astype(bf16).reshape(chips, CAP, width_ch)
+
+        for q in range(4):
+
+            def dispatch(slot, dz, dx):
+                to = place.at(dz, dx)
+                for k in range(2 * side, 2 * side + 2):
+                    remote(
+                        send.at[k * chips + to], got.at[y * chips + slot], send_sem, got_sem.at[q],
+                        ctx=to * 2 + core, ch=k,
+                    ).start()
+
+            each(q, dispatch)
+            for k in range(2 * side, 2 * side + 2) if q == 0 else ():
+
+                @pl.when(y != k)
+                def _():
+                    remote(
+                        send.at[k * chips + chip], got.at[y * chips + 7], send_sem, got_sem.at[0], ch=k
+                    ).start()
+
+                pl.when(y == k)(keep.start)
+
     keep_back = pltpu.make_async_copy(summed.at[y * chips + 7], back.at[mine], local_sem.at[1])
     whole.wait_send()
-    whole_back.wait_send()
+    for back_half, _ in returns:
+        back_half.wait_send()
     for swap in swaps:
         swap.wait()
     column = router_t[pl.ds(chip, 1), :]
@@ -367,13 +390,13 @@
         scratch_shapes=[vmem(a.shape, a.dtype) for a in far[:-2]]
         + [vmem((shards, 2 * chans, tok_dev), bf16)] * 2
         + [vmem((2 * chans * shards, tok_dev), bf16)] * 2
-        + [vmem((shards, 2 * chans, tok_dev // 2), bf16)] * 2
+        + [vmem((2, shards, 2 * chans, tok_dev // 4), bf16)] * 2
         + [vmem((groups, 2, rows), routes.dtype)]
         + [vmem(blocks, bf16)]
         + [vmem((groups, experts * CAP, rows), bf16)]
         + [vmem(blocks, bf16)] * 3
         + [vmem((2, width, hidden), bf16), vmem((2, hidden, width), bf16)]
-        + [dma((12,)), dma((3,)), dma((4,)), dma((3,)), dma((3,)), dma]
+        + [dma((12,)), dma((5,)), dma((6,)), dma((3,)), dma((3,)), dma]
         + [dma((4,)), dma((2,)), dma((2,)), dma, dma],
         compiler_params=pltpu.CompilerParams(collective_id=0, has_side_effects=True),
     )(skip[None, :], norm_gain[None, :], routes.T, *far)

time: 94.5 us -> 91.3 us (0.966)
  Pallas kernels: 93.7 us -> 90.5 us
    pallas_call x1, Pallas kernels: 91.9 us -> 88.7 us  [body(): pl.pallas_call(layer_kernel, out_shape=(local, local), in_specs=[here] *...]
where the time goes in v8:
time: 91.3 us; the launch traced here: 91.2 us
  Pallas kernels  90.5 us (99%)
    pallas_call x1, Pallas kernels, body(): pl.pallas_call(layer_kernel, out_shape=(local, local), in_specs=[here] *...  88.7 us
    pallas_call x1, Pallas kernels, body(): pl.pallas_call(publish_kernel, out_shape=(local, local), in_specs=[here]...  1.84 us

profile of v8, /device:TPU:1, one launch (start us, length us, event | category | flops | bytes accessed | tf_op | source)
XLA Modules:
  0.0 91.2 jit_solution(5193896815519412560)
XLA Ops:
  0.6 88.7 %shard_map.158 = (bf16[512,256]{1,0:T(8,128)(2,1)}, bf16[512,256]{1,0:T(8,128)(2,1)}) custom-call(f32[1,256]{1,0:T(1,128)} %bitcast.10, f32[1,1024]{1,0:T(1,128)} %bitcast.9, s32[2,128]{1,0:T(2,128)} %bitcast.11, bf16[512,256]{1,0:T(8,128)(2,1)} %rest_0_.1, f32[512,256]{1,0:T(8,128)} %rest_1_.1, bf16[512,256]{1,0:T(8,128)(2,1)} %rest_2_.1, ...), custom_call_target="tpu_custom_call" | custom-call | tf_op jit(solution)/shard_map/pallas_call | solution.py:385
  89.3 1.8 %shard_map.159 = (bf16[512,256]{1,0:T(8,128)(2,1)}, bf16[512,256]{1,0:T(8,128)(2,1)}) custom-call(bf16[512,256]{1,0:T(8,128)(2,1)} %get-tuple-element.4.a_ref, bf16[512,256]{1,0:T(8,128)(2,1)} %get-tuple-element.5.b_ref), custom_call_target="tpu_custom_call" | custom-call | tf_op jit(solution)/shard_map/pallas_call | solution.py:404

commit v9 on v8

--- a/solution.py
+++ b/solution.py
@@ -80,27 +80,27 @@
     half = chans * shards
     p_re = (x_re[:half] * x_re[half:] - x_im[:half] * x_im[half:]).astype(bf16)
     p_im = (x_re[:half] * x_im[half:] + x_im[:half] * x_re[half:]).astype(bf16)
+    return p_re, p_im
+
+
+def last_step(product, tables, side, shards, chans):
+    p_re, p_im = product
+    count = tables[1].shape[1] // 4
+    span = pl.ds(2 * side * count, 2 * count)
+    tr, ti, cos, sin = (table[:, span] for table in tables[1:5])
+    last = tables[5][...]
     g_re = dot(p_re, cos) - dot(p_im, sin)
     g_im = dot(p_im, cos) + dot(p_re, sin)
-    pairs = []
+    row = iota(last.shape, 0) % (2 * chans)
+    total = jnp.zeros((last.shape[0], count), f32)
     for chan in range(chans):
         rows = slice(chan * shards, (chan + 1) * shards)
         a = (g_re[rows] * tr + g_im[rows] * ti).astype(bf16)
         b = (g_im[rows] * tr - g_re[rows] * ti).astype(bf16)
-        pairs.append(jnp.concatenate([a, b], axis=0))
-    return pairs
-
-
-def last_step(pairs, last, side):
-    chans = len(pairs)
-    row = iota(last.shape, 0) % (2 * chans)
-    count = pairs[0].shape[1] // 4
-    total = jnp.zeros((last.shape[0], count), f32)
-    for chan, pair in enumerate(pairs):
+        pair = jnp.concatenate([a, b], axis=0)
         for part in range(2):
             table = jnp.where(row == part * chans + chan, last, jnp.zeros_like(last))
-            start = (2 * side + part) * count
-            total += dot(table, pair[:, start : start + count])
+            total += dot(table, pair[:, part * count : (part + 1) * count])
     return total
 
 
@@ -161,11 +161,14 @@
     def tell(**where):
         pl.semaphore_signal(barrier, inc=1, device_id=where, device_id_type=pl.DeviceIdType.MESH)
 
+    tell(ctx=(place.me + count // 2) % count)
+
     def shard(i, carry):
-        tell(ctx=(place.me + i) % count)
+        tell(ctx=(place.me + count // 2 + i) % count)
+        tell(ctx=(place.me + count // 2 - i) % count)
         return carry
 
-    lax.fori_loop(1, count, shard, 0)
+    lax.fori_loop(1, count // 2, shard, 0)
     for dy in range(1, ys):
         tell(ch=(place.y + dy) % ys)
     return lambda: pl.semaphore_wait(barrier, count - 1 + ys - 1)
@@ -204,9 +207,9 @@
     (
         far, (mixed_out, out),
         near, (packed, fields, re_ref, im_ref, conv_out, conv_in, routes_all),
-        (send, here, got, summed, back, ups, downs),
+        (send, here, turned, got, summed, back, ups, downs),
         (far_sem, local_sem, conv_sem, xs_sem, xr_sem, send_sem, got_sem, ws_sem, wr_sem, rs_sem, back_sem),
-    ) = split(rest, (12, 2, 10, 7, 7, 11))
+    ) = split(rest, (12, 2, 10, 7, 8, 11))
     shards, width_ch = 64, near[0].shape[1]
     chans = width_ch // shards
     chips, groups, chunk = 32, 4, 8
@@ -267,10 +270,11 @@
     for swap in swaps:
         swap.start()
     data = fields[...].astype(f32).reshape(shards * 2 * chans, -1).astype(bf16)
-    pairs = convolve(data, tables, re_ref, im_ref, shards, chans)
+    product = convolve(data, tables, re_ref, im_ref, shards, chans)
     returns = []
     for side in range(2):
-        conv_out[side] = last_step(pairs, tables[5][...], side).reshape(conv_out.shape[1:]).astype(bf16)
+        total = last_step(product, tables, side, shards, chans)
+        conv_out[side] = total.reshape(conv_out.shape[1:]).astype(bf16)
         returns.append(
             spread_out(
                 conv_out.at[side], conv_in.at[side], conv_sem.at[2 + 2 * side], conv_sem.at[3 + 2 * side],
@@ -320,6 +324,10 @@
     for swap in swaps:
         swap.wait()
     column = router_t[pl.ds(chip, 1), :]
+    count = here.shape[2]
+    turn = one_hot(iota((count, count), 0) == iota((count, count), 1))
+    for k in range(groups):
+        turned[k] = contract(turn, here[k], 1, 1).astype(bf16)
     for q in range(4):
         came = pl.ds(0, groups * chunk - (q == 0))
         remote(send.at[came], got.at[came], send_sem, got_sem.at[q], ctx=me).wait_recv()
@@ -357,7 +365,7 @@
     remote(summed.at[others], back.at[others], rs_sem, back_sem, ctx=me).wait_recv()
     for k in range(groups):
         slots = back[k * chips : (k + 1) * chips].reshape(chips * CAP, width_ch)
-        rows = contract(here[k], slots, 0, 0).astype(bf16)
+        rows = dot(turned[k], slots).astype(bf16)
         out[k * rows.shape[0] : (k + 1) * rows.shape[0], :] = rows
     remote(send.at[others], got.at[others], send_sem, got_sem.at[0], ctx=me).wait_send()
     remote(summed.at[others], back.at[others], rs_sem, back_sem, ctx=me).wait_send()
@@ -393,7 +401,7 @@
         + [vmem((2, shards, 2 * chans, tok_dev // 4), bf16)] * 2
         + [vmem((groups, 2, rows), routes.dtype)]
         + [vmem(blocks, bf16)]
-        + [vmem((groups, experts * CAP, rows), bf16)]
+        + [vmem((groups, experts * CAP, rows), bf16), vmem((groups, rows, experts * CAP), bf16)]
         + [vmem(blocks, bf16)] * 3
         + [vmem((2, width, hidden), bf16), vmem((2, hidden, width), bf16)]
         + [dma((12,)), dma((5,)), dma((6,)), dma((3,)), dma((3,)), dma]

time: 91.3 us -> 91 us (level)
  no operation moved by 1% of the time
where the time goes in v9:
time: 91 us; the launch traced here: 90.8 us
  Pallas kernels  90.2 us (99%)
    pallas_call x1, Pallas kernels, body(): pl.pallas_call(layer_kernel, out_shape=(local, local), in_specs=[here] *...  88.3 us
    pallas_call x1, Pallas kernels, body(): pl.pallas_call(publish_kernel, out_shape=(local, local), in_specs=[here]...  1.84 us

profile of v9, /device:TPU:1, one launch (start us, length us, event | category | flops | bytes accessed | tf_op | source)
XLA Modules:
  0.0 90.8 jit_solution(18019373502187740678)
XLA Ops:
  0.6 88.3 %shard_map.158 = (bf16[512,256]{1,0:T(8,128)(2,1)}, bf16[512,256]{1,0:T(8,128)(2,1)}) custom-call(f32[1,256]{1,0:T(1,128)} %bitcast.10, f32[1,1024]{1,0:T(1,128)} %bitcast.9, s32[2,128]{1,0:T(2,128)} %bitcast.11, bf16[512,256]{1,0:T(8,128)(2,1)} %rest_0_.1, f32[512,256]{1,0:T(8,128)} %rest_1_.1, bf16[512,256]{1,0:T(8,128)(2,1)} %rest_2_.1, ...), custom_call_target="tpu_custom_call" | custom-call | tf_op jit(solution)/shard_map/pallas_call | solution.py:393
  89.0 1.8 %shard_map.159 = (bf16[512,256]{1,0:T(8,128)(2,1)}, bf16[512,256]{1,0:T(8,128)(2,1)}) custom-call(bf16[512,256]{1,0:T(8,128)(2,1)} %get-tuple-element.4.a_ref, bf16[512,256]{1,0:T(8,128)(2,1)} %get-tuple-element.5.b_ref), custom_call_target="tpu_custom_call" | custom-call | tf_op jit(solution)/shard_map/pallas_call | solution.py:412

commit v10 on v9

--- a/solution.py
+++ b/solution.py
@@ -296,7 +296,7 @@
             mixed_out[span, :] = value
             send[k * chips : (k + 1) * chips] = dot(here[k], value).astype(bf16).reshape(chips, CAP, width_ch)
 
-        for q in range(4):
+        for q in (0, 3, 2, 1):
 
             def dispatch(slot, dz, dx):
                 to = place.at(dz, dx)
@@ -328,7 +328,7 @@
     turn = one_hot(iota((count, count), 0) == iota((count, count), 1))
     for k in range(groups):
         turned[k] = contract(turn, here[k], 1, 1).astype(bf16)
-    for q in range(4):
+    for q in (0, 3, 2, 1):
         came = pl.ds(0, groups * chunk - (q == 0))
         remote(send.at[came], got.at[came], send_sem, got_sem.at[q], ctx=me).wait_recv()
         if q == 0:

time: 91 us -> 89.7 us (0.986)
  Pallas kernels: 90.2 us -> 88.4 us
    pallas_call x1, Pallas kernels: 88.3 us -> 86.6 us  [body(): pl.pallas_call(layer_kernel, out_shape=(local, local), in_specs=[here] *...]
where the time goes in v10:
time: 89.7 us; the launch traced here: 89 us
  Pallas kernels  88.4 us (99%)
    pallas_call x1, Pallas kernels, body(): pl.pallas_call(layer_kernel, out_shape=(local, local), in_specs=[here] *...  86.6 us
    pallas_call x1, Pallas kernels, body(): pl.pallas_call(publish_kernel, out_shape=(local, local), in_specs=[here]...  1.84 us

profile of v10, /device:TPU:1, one launch (start us, length us, event | category | flops | bytes accessed | tf_op | source)
XLA Modules:
  0.0 89.0 jit_solution(17690325707665594289)
XLA Ops:
  0.6 86.6 %shard_map.158 = (bf16[512,256]{1,0:T(8,128)(2,1)}, bf16[512,256]{1,0:T(8,128)(2,1)}) custom-call(f32[1,256]{1,0:T(1,128)} %bitcast.10, f32[1,1024]{1,0:T(1,128)} %bitcast.9, s32[2,128]{1,0:T(2,128)} %bitcast.11, bf16[512,256]{1,0:T(8,128)(2,1)} %rest_0_.1, f32[512,256]{1,0:T(8,128)} %rest_1_.1, bf16[512,256]{1,0:T(8,128)(2,1)} %rest_2_.1, ...), custom_call_target="tpu_custom_call" | custom-call | tf_op jit(solution)/shard_map/pallas_call | solution.py:393
  87.2 1.8 %shard_map.159 = (bf16[512,256]{1,0:T(8,128)(2,1)}, bf16[512,256]{1,0:T(8,128)(2,1)}) custom-call(bf16[512,256]{1,0:T(8,128)(2,1)} %get-tuple-element.4.a_ref, bf16[512,256]{1,0:T(8,128)(2,1)} %get-tuple-element.5.b_ref), custom_call_target="tpu_custom_call" | custom-call | tf_op jit(solution)/shard_map/pallas_call | solution.py:412

commit v11 on v10

--- a/solution.py
+++ b/solution.py
@@ -296,7 +296,7 @@
             mixed_out[span, :] = value
             send[k * chips : (k + 1) * chips] = dot(here[k], value).astype(bf16).reshape(chips, CAP, width_ch)
 
-        for q in (0, 3, 2, 1):
+        for q in (3, 0, 2, 1):
 
             def dispatch(slot, dz, dx):
                 to = place.at(dz, dx)
@@ -328,7 +328,7 @@
     turn = one_hot(iota((count, count), 0) == iota((count, count), 1))
     for k in range(groups):
         turned[k] = contract(turn, here[k], 1, 1).astype(bf16)
-    for q in (0, 3, 2, 1):
+    for q in (3, 0, 2, 1):
         came = pl.ds(0, groups * chunk - (q == 0))
         remote(send.at[came], got.at[came], send_sem, got_sem.at[q], ctx=me).wait_recv()
         if q == 0:

time: 89.7 us -> 90 us (level)
  no operation moved by 1% of the time
where the time goes in v11:
time: 90 us; the launch traced here: 89.9 us
  Pallas kernels  89.2 us (99%)
    pallas_call x1, Pallas kernels, body(): pl.pallas_call(layer_kernel, out_shape=(local, local), in_specs=[here] *...  87.4 us
    pallas_call x1, Pallas kernels, body(): pl.pallas_call(publish_kernel, out_shape=(local, local), in_specs=[here]...  1.84 us

profile of v11, /device:TPU:1, one launch (start us, length us, event | category | flops | bytes accessed | tf_op | source)
XLA Modules:
  0.0 89.9 jit_solution(7171733918692438032)
XLA Ops:
  0.6 87.4 %shard_map.158 = (bf16[512,256]{1,0:T(8,128)(2,1)}, bf16[512,256]{1,0:T(8,128)(2,1)}) custom-call(f32[1,256]{1,0:T(1,128)} %bitcast.10, f32[1,1024]{1,0:T(1,128)} %bitcast.9, s32[2,128]{1,0:T(2,128)} %bitcast.11, bf16[512,256]{1,0:T(8,128)(2,1)} %rest_0_.1, f32[512,256]{1,0:T(8,128)} %rest_1_.1, bf16[512,256]{1,0:T(8,128)(2,1)} %rest_2_.1, ...), custom_call_target="tpu_custom_call" | custom-call | tf_op jit(solution)/shard_map/pallas_call | solution.py:393
  88.0 1.8 %shard_map.159 = (bf16[512,256]{1,0:T(8,128)(2,1)}, bf16[512,256]{1,0:T(8,128)(2,1)}) custom-call(bf16[512,256]{1,0:T(8,128)(2,1)} %get-tuple-element.4.a_ref, bf16[512,256]{1,0:T(8,128)(2,1)} %get-tuple-element.5.b_ref), custom_call_target="tpu_custom_call" | custom-call | tf_op jit(solution)/shard_map/pallas_call | solution.py:412
